TPU v7x, 32 devices: a whole 2x2x4 slice. The times are simulated.
32 devices in a mesh: dp: 8 (over z, y), tensor: 4 (over x, core).
Axes of the slice: x: 2, y: 2, z: 4, core: 2. Of those that a mesh axis runs over, the one named last changes fastest.
Arguments:
- tokens: bfloat16 [8192, 1024], P(('dp', 'tensor')), may hold values from -6 to 6
- cotangent: float32 [8192, 1024], P(('dp', 'tensor')), may hold values from -6 to 6
- lengths: int32 [8, 2], P('dp'), may hold values from 64 to 512, as said below
- order: int32 [8, 1024], P('dp'), may hold values from 0 to 1023, each once within a row
- adapter_ids: int32 [8, 2], P('dp'), may hold values from 0 to 7
- norm1_gain: float32 [1024], replicated, may hold values from 0.25 to 1.75
- norm1_shift: float32 [1024], replicated, may hold values from -1.5 to 1.5
- qkv_weight: bfloat16 [1024, 3, 1024], P(None, None, 'tensor'), may hold values from -0.1875 to 0.1875
- qv_bias: float32 [2, 1024], P(None, 'tensor'), may hold values from -1.5 to 1.5
- proj_weight: bfloat16 [1024, 1024], P('tensor'), may hold values from -1.5 to 1.5
- proj_bias: float32 [1024], replicated, may hold values from -1.5 to 1.5
- norm2_gain: float32 [1024], replicated, may hold values from 0.25 to 1.75
- norm2_shift: float32 [1024], replicated, may hold values from -1.5 to 1.5
- up_weight: bfloat16 [1024, 4096], P(None, 'tensor'), may hold values from -0.1875 to 0.1875
- up_bias: float32 [4096], P('tensor'), may hold values from -1.5 to 1.5
- down_weight: bfloat16 [4096, 1024], P('tensor'), may hold values from -0.09375 to 0.09375
- down_bias: float32 [1024], replicated, may hold values from -1.5 to 1.5
- adapt_qkv_in: bfloat16 [1024, 128], replicated, may hold values from -0.1875 to 0.1875
- adapt_qkv_out: bfloat16 [128, 3, 1024], P(None, None, 'tensor'), may hold values from -0.75 to 0.75
- adapt_proj_in: bfloat16 [1024, 128], P('tensor'), may hold values from -0.75 to 0.75
- adapt_proj_out: bfloat16 [128, 1024], replicated, may hold values from -0.75 to 0.75
- adapt_up_in: bfloat16 [1024, 128], replicated, may hold values from -0.1875 to 0.1875
- adapt_up_out: bfloat16 [128, 4096], P(None, 'tensor'), may hold values from -0.75 to 0.75
- adapt_down_in: bfloat16 [4096, 128], P('tensor'), may hold values from -0.09375 to 0.09375
- adapt_down_out: bfloat16 [128, 1024], replicated, may hold values from -0.75 to 0.75
Outputs:
- result: float32 [8192, 1024], P(('dp', 'tensor'))
- grad_input: float32 [8192, 1024], P(('dp', 'tensor'))
- grad_qkv_in: float32 [1024, 128], replicated
- grad_qkv_out: float32 [128, 3, 1024], P(None, None, 'tensor')
- grad_proj_in: float32 [1024, 128], P('tensor')
- grad_proj_out: float32 [128, 1024], replicated
- grad_up_in: float32 [1024, 128], replicated
- grad_up_out: float32 [128, 4096], P(None, 'tensor')
- grad_down_in: float32 [4096, 128], P('tensor')
- grad_down_out: float32 [128, 1024], replicated
Inputs may be any that keep to these rules, and one draw needn't show every extreme that they name: `lengths`: in every group one sequence has exactly 512 valid tokens; the others have at least 512 // 8 (and at least one). `order`: each row is a permutation of the group's 1024 stored rows.
All inputs are finite; a program needn't handle non-finite values.
Results may differ from a plain program's by a relative error of at most 0.023.
Values may be sent and summed in bfloat16 or wider, within the bound.
No kernel may reach another device: no remote copies, remote signals or barrier semaphores. Data moves between devices by JAX's collectives and lax.ppermute only.
A program may use at most 128 MiB of HBM per device.

v0:
```python
import functools
import math

import jax
import jax.numpy as jnp
from jax import lax
from jax.experimental import pallas as pl
from jax.experimental.pallas import tpu as pltpu
from jax.sharding import PartitionSpec as P

HD = 64
RANK = 16
PAIR = 2 * HD
EPSILON = 1e-05
NEGATIVE = -1000000000.0
BF = jnp.bfloat16
F32 = jnp.float32
LIMIT = 10 * 1024 * 1024
GELU_A = math.sqrt(2.0 / math.pi)
GELU_B = 0.044715


def dot(left, right):
    return jnp.dot(left, right, preferred_element_type=F32)


def dot_back(left, right):
    return lax.dot_general(left, right, (((1,), (1,)), ((), ())), preferred_element_type=F32)


def dot_over(left, right):
    return lax.dot_general(left, right, (((0,), (0,)), ((), ())), preferred_element_type=F32)


def shape(dims, kind):
    return jax.ShapeDtypeStruct(tuple(dims), kind)


def whole_call(body, inputs, outs, name, smem=(), scratch=(), final=(), loose=(), long=False):
    smem_spec = pl.BlockSpec(memory_space=pltpu.SMEM)
    vmem_spec = pl.BlockSpec(memory_space=pltpu.VMEM)
    held = [
        pltpu.with_memory_space_constraint(x, pltpu.HBM if i in loose else pltpu.VMEM) for i, x in enumerate(inputs)
    ]
    kinds = [o if i in final else pltpu.VMEM(o.shape, o.dtype) for i, o in enumerate(outs)]
    return pl.pallas_call(
        body,
        out_shape=kinds,
        in_specs=[smem_spec] * len(smem) + [vmem_spec] * len(inputs),
        out_specs=[vmem_spec] * len(outs),
        scratch_shapes=list(scratch),
        compiler_params=pltpu.CompilerParams(vmem_limit_bytes=LIMIT),
        name=name,
    )(*smem, *held)


def norm_parts(values):
    centre = values - jnp.mean(values, -1, keepdims=True)
    spread = jnp.mean(centre * centre, -1, keepdims=True)
    inv = lax.rsqrt(spread + EPSILON)
    return centre * inv, inv


def norm_back(normed, inv, upstream):
    return inv * (
        upstream
        - jnp.mean(upstream, -1, keepdims=True)
        - normed * jnp.mean(upstream * normed, -1, keepdims=True)
    )


def rows_at(i, size):
    return pl.ds(pl.multiple_of(i * size, size), size)


def repeat(count, step):
    if count == 1:
        step(0)
    else:
        lax.fori_loop(0, count, lambda i, carry: (step(i), carry)[1], 0)


def owner_of(me, d, count):
    return (((me // 2) + count // 2 - d // 2) % (count // 2)) * 2 + ((me % 2 + d % 2) % 2)


def prep_body(
    seq_len, own, count, me, dp_at, lengths, ids, order, proj_w, qkv_in, qkv_out, proj_in, proj_out, up_in, up_out,
    down_in, down_out, *outs
):
    o_qkv_in, o_qkv_out, o_proj, o_proj_out, o_up_in, o_up_out, o_down_in, o_down_out = outs[:8]
    pull_near, pull_far, push, mask, pick, limit, o_half, tall_ref = outs[8:]
    rank_at = lax.broadcasted_iota(jnp.int32, pick.shape, 0)
    col_at = lax.broadcasted_iota(jnp.int32, pick.shape, 1)
    wanted = rank_at + ids[0, 0] * RANK
    slot = lax.broadcasted_iota(jnp.int32, limit.shape, 1)
    bound = jnp.minimum(slot + 1, lengths[0, 0])
    for s in range(1, lengths.shape[1]):
        wanted = jnp.where(rank_at >= s * RANK, rank_at - s * RANK + ids[0, s] * RANK, wanted)
        bound = jnp.where(slot >= s * seq_len, jnp.minimum(slot - s * seq_len + 1, lengths[0, s]), bound)
    limit[...] = bound
    chosen = jnp.where(col_at == wanted, 1.0, 0.0).astype(BF)
    pick[...] = chosen
    width = proj_w.shape[0]
    fold = pick.shape[0] // count
    o_proj[pl.ds(0, width), :] = proj_w[...]
    o_proj[pl.ds(width, 16), :] = jnp.zeros((16, o_proj.shape[1]), BF)
    chosen_in = dot_back(chosen, proj_in[...])
    for j in range(count):
        o_proj[pl.ds(width, fold), j * width : (j + 1) * width] = chosen_in[j * fold : (j + 1) * fold].astype(BF)
    half = width // 2
    o_half[pl.ds(0, half), :] = proj_w[pl.ds(pl.multiple_of(dp_at[0] % 2 * half, half), half), :]
    o_half[pl.ds(half, 16), :] = o_proj[pl.ds(width, 16), :]
    o_qkv_in[...] = dot_back(chosen, qkv_in[...]).astype(BF)
    for k in range(3):
        o_qkv_out[k] = dot(chosen, qkv_out[k]).astype(BF)
    o_proj_out[...] = dot(chosen, proj_out[...]).astype(BF)
    o_up_in[...] = dot_back(chosen, up_in[...]).astype(BF)
    o_up_out[...] = dot(chosen, up_out[...]).astype(BF)
    o_down_in[...] = dot_back(chosen, down_in[...]).astype(BF)
    o_down_out[...] = dot(chosen, down_out[...]).astype(BF)
    stored = order[...]
    relative = stored
    for d in range(count):
        start = owner_of(me[0], d, count) * own
        relative = jnp.where((stored >= start) & (stored < start + own), stored - start + d * own, relative)
    near = pull_near.shape[1]
    rows = push.shape[0]
    tall = jnp.broadcast_to(relative.astype(F32), (8, rows)).T[:, :1].astype(jnp.int32)
    tall_ref[...] = tall

    def one_hot(i):
        part = rows_at(i, own)
        for ref, start in ((pull_near, 0), (pull_far, near)):
            at = lax.broadcasted_iota(jnp.int32, (own, ref.shape[1]), 1) + start
            ref[part, :] = jnp.where(at == tall_ref[part, :], 1.0, 0.0).astype(BF)
        at = lax.broadcasted_iota(jnp.int32, (own, rows), 0) + i * own
        push[part, :] = jnp.where(at == relative, 1.0, 0.0).astype(BF)

    repeat(rows // own, one_hot)
    seq_at = lax.broadcasted_iota(jnp.int32, mask.shape, 0) // seq_len
    lane_at = lax.broadcasted_iota(jnp.int32, mask.shape, 1) // RANK
    mask[...] = dot(push[...], jnp.where(seq_at == lane_at, 1.0, 0.0).astype(BF))


def qkv_body(ids, last, mask, gain, shift, weight, bias, low_in, low_out, pull, *refs):
    count = len(ids)
    blocks = refs[:count]
    rest = refs[count:]
    earlier = None
    if last:
        earlier, rest = rest[0], rest[1:]
    normed_ref, low_ref, moved_ref, joined, tokens, keep = rest
    rows = blocks[0].shape[0]
    width = weight.shape[2]
    for i in range(count):
        tokens[pl.ds(i * rows, rows), :] = blocks[i][...]
        keep[pl.ds(i * rows, rows), :] = mask[pl.ds(ids[i] * rows, rows), :]

    def project(i):
        part = rows_at(i, rows)
        unit, _ = norm_parts(tokens[part, :].astype(F32))
        normed = (unit * gain[...] + shift[...]).astype(BF)
        normed_ref[part, :] = normed
        low = (dot_back(normed, low_in[...]) * keep[part, :]).astype(BF)
        low_ref[part, :] = low
        for k in range(3):
            value = dot(normed, weight[k]) + dot(low, low_out[k])
            if k != 1:
                value = value + bias[k // 2 : k // 2 + 1, :]
            joined[part, k * width : (k + 1) * width] = value.astype(BF)

    repeat(count, project)
    total = moved_ref.shape[0]
    step = min(256, total)

    def move(i):
        part = rows_at(i, step)
        moved = dot(pull[part, :], joined[...])
        if last:
            moved = moved + earlier[part, :]
            moved_ref[part, :width] = (moved[:, :width] * (1.0 / math.sqrt(HD))).astype(BF)
            moved_ref[part, width:] = moved[:, width:].astype(BF)
        else:
            moved_ref[part, :] = moved

    repeat(total // step, move)


def head_lanes(values, head):
    lane = lax.broadcasted_iota(jnp.int32, values.shape, 1)
    return jnp.where((lane // HD) == head, values, jnp.zeros_like(values))


def attend_body(seq_len, pair, limit, seq, push, out, kept, turned):
    rows = seq.shape[0]
    width = seq.shape[1] // 3
    step = min(256, seq_len)

    def one(s):
        base = s * seq_len
        all_rows = rows_at(s, seq_len)
        keys = seq[all_rows, pl.ds(width + pair * PAIR, PAIR)]
        values = seq[all_rows, pl.ds(2 * width + pair * PAIR, PAIR)]
        values_t = values.astype(F32).T.astype(BF)
        for q in range(seq_len // step):
            span = pl.ds(pl.multiple_of(base + q * step, step), step)
            queries = seq[span, pl.ds(pair * PAIR, PAIR)]
            seen = (q + 1) * step
            allowed = lax.broadcasted_iota(jnp.int32, (seen, step), 0) < limit[:, span]
            for h in range(2):
                scores = dot_back(keys[:seen], head_lanes(queries, h))
                scores = jnp.where(allowed, scores, NEGATIVE)
                weights = jnp.exp(scores - jnp.max(scores, 0, keepdims=True))
                total = jnp.sum(weights, 0, keepdims=True)
                probs = (weights * (1.0 / total)).astype(BF)
                kept[s, h, :seen, q * step : (q + 1) * step] = probs
                turned[pl.ds(h * HD, HD), span] = dot(values_t[h * HD : (h + 1) * HD, :seen], probs).astype(BF)

    repeat(rows // seq_len, one)
    out[...] = dot_back(push[...], turned[...]).astype(BF)


def join_body(count, dp_at, low_near, low_far, push, weight, *refs):
    proj = refs[:2]
    parts = refs[2 : 2 + 2 * (count - 2)]
    w_all, in_all, w_cat, low_t = refs[2 + 2 * (count - 2) :]
    width = in_all.shape[1] // count
    half = width // 2
    fold = in_all.shape[0] // count
    near = low_near.shape[0]
    for d in range(count):
        if d < 2:
            source, at = proj[d], width
            w_all[pl.ds(d * width, width), :] = source[pl.ds(0, width), :]
        else:
            source, at = parts[2 * (d - 2)], half
            start = pl.multiple_of(dp_at[0] % 2 * half, half)
            w_all[pl.ds(d * width + start, half), :] = source[pl.ds(0, half), :]
            start = pl.multiple_of((dp_at[0] + 1) % 2 * half, half)
            w_all[pl.ds(d * width + start, half), :] = parts[2 * (d - 2) + 1][...]
        for j in range(count):
            part = source[pl.ds(at, fold), j * width : (j + 1) * width]
            in_all[pl.ds(j * fold, fold), d * width : (d + 1) * width] = part
    for k in range(3):
        w_cat[:, k * width : (k + 1) * width] = weight[k]
    rows = push.shape[0]
    low_t[...] = (
        dot_over(low_near[...], push[pl.ds(0, near), :]) + dot_over(low_far[...], push[pl.ds(near, rows - near), :])
    ).astype(BF)


def place_of(block, sender, chips):
    return ((block // 2 - sender // 2) % chips) * 2 + ((block % 2) ^ (sender % 2))


def block_body(
    ids, count, pairs, chunk, mask, w_all, in_all, proj_out, proj_bias, gain, shift, up_in, up_w, up_b, up_out,
    down_w, down_in, down_out, *refs
):
    size = len(ids)
    tokens = refs[:size]
    grads = refs[size : 2 * size]
    attended = refs[2 * size : 2 * size + count * pairs]
    rest = refs[2 * size + count * pairs :]
    outs = rest[: len(rest) - 7]
    heads, grad_all, token_all, keep_all, acc, low_acc, down_acc = rest[len(rest) - 7 :]
    part_ref, normed_ref, low_ref, low_part, grad_down_low, act_ref, gup_ref, down_low = outs[:8]
    block = tokens[0].shape[0]
    width = in_all.shape[1] // count
    for i in range(size):
        part = pl.ds(i * block, block)
        for d in range(count):
            spot = place_of(ids[i], d, count // 2) * block
            for p in range(pairs):
                at = d * width + p * PAIR
                heads[part, at : at + PAIR] = attended[d * pairs + p][pl.ds(spot, block), :]
        keep_all[part, :] = mask[pl.ds(ids[i] * block, block), :]
        grad_all[part, :] = grads[i][...]
        token_all[part, :] = tokens[i][...]

    def one(i):
        part = rows_at(i, block)
        keep = keep_all[part, :]
        grad = grad_all[part, :]
        grad_low = (dot_back(grad, down_out[...]) * keep).astype(BF)
        grad_down_low[part, :] = grad_low
        rows = heads[part, :]
        low = (dot_back(rows, in_all[...]) * keep).astype(BF)
        mid = dot(rows, w_all[...]) + dot(low, proj_out[...]) + proj_bias[...] + token_all[part, :].astype(F32)
        unit, _ = norm_parts(mid)
        normed = (unit * gain[...] + shift[...]).astype(BF)
        normed_ref[part, :] = normed
        low2 = (dot_back(normed, up_in[...]) * keep).astype(BF)
        low_ref[part, :] = low2
        if len(outs) > 8:
            outs[8][part, :] = low
            outs[9][part, :] = mid
        acc[...] = jnp.zeros_like(acc)
        low_acc[...] = jnp.zeros_like(low_acc)
        down_acc[...] = jnp.zeros_like(down_acc)

        def one_chunk(j):
            cut = rows_at(j, chunk)
            upper = dot(normed, up_w[:, cut]) + dot(low2, up_out[:, cut]) + up_b[:, cut]
            grad_act = dot_back(grad, down_w[cut, :]) + dot(grad_low, down_in[:, cut])
            square = upper * upper
            curve = jnp.tanh(GELU_A * upper * (1.0 + GELU_B * square))
            half = 0.5 * (1.0 + curve)
            active = (upper * half).astype(BF)
            act_ref[part, cut] = active
            slope = half + 0.5 * upper * (1.0 - curve * curve) * (GELU_A * (1.0 + 3.0 * GELU_B * square))
            grad_upper = (grad_act * slope).astype(BF)
            gup_ref[part, cut] = grad_upper
            acc[...] += dot_back(grad_upper, up_w[:, cut])
            low_acc[...] += dot_back(grad_upper, up_out[:, cut])
            down_acc[...] += dot_back(active, down_in[:, cut])

        repeat(up_w.shape[1] // chunk, one_chunk)
        low = (low_acc[...] * keep).astype(BF)
        low_part[part, :] = low
        down_low[part, :] = (down_acc[...] * keep).astype(BF)
        part_ref[part, :] = (acc[...] + dot(low, up_in[...])).astype(BF)

    repeat(size, one)


def down_body(groups, block, down_w, down_out, *refs):
    for g in range(groups):
        act, low, out = refs[g], refs[groups + g], refs[2 * groups + g]

        def one(i, act=act, low=low, out=out):
            part = rows_at(i, block)
            out[part, :] = (dot(act[part, :], down_w[...]) + dot(low[part, :], down_out[...])).astype(BF)

        repeat(act.shape[0] // block, one)


def hidden_grads_body(groups, sizes, pick, *refs):
    low2 = refs[:groups]
    gup = refs[groups : 2 * groups]
    gdl = refs[2 * groups : 3 * groups]
    act = refs[3 * groups : 4 * groups]
    part = refs[4 * groups : 5 * groups]
    normed = refs[5 * groups : 6 * groups]
    down = refs[6 * groups : 7 * groups]
    rest = refs[7 * groups :]
    total = sum(sizes)
    grads = rest[:total]
    pack, up_in, down_out = rest[total:]
    hid = gup[0].shape[1]
    block = grads[0].shape[0]
    add = lambda left, right: sum([dot_over(a[...], b[...]) for a, b in zip(left[1:], right[1:])], dot_over(left[0][...], right[0][...]))
    pack[:, :hid] = add(low2, gup).astype(BF)
    pack[:, hid : 2 * hid] = add(gdl, act).astype(BF)
    pack[:, 2 * hid :] = pick[...]
    up_in[...] = add(part, normed)
    at = 0
    out = None
    for g in range(groups):
        for i in range(sizes[g]):
            term = dot_over(down[g][pl.ds(i * block, block), :], grads[at][...])
            out = term if out is None else out + term
            at += 1
    down_out[...] = out


def add_body(left, right, out):
    out[...] = (left[...].astype(F32) + right[...].astype(F32)).astype(BF)


def mid_back_body(count, mask, cotangent, mid, gain, proj_out, w_all, in_all, *refs):
    pieces = refs[: count[0]]
    grad_mid, grad_attn, grad_low = refs[count[0] : count[0] + 3]
    outs = refs[count[0] + 3 :]
    width = outs[0].shape[1]
    half = cotangent.shape[0] // 2

    def one(i):
        part = rows_at(i, half)
        upstream = pieces[0][part, :].astype(F32)
        for piece in pieces[1:]:
            upstream = upstream + piece[part, :].astype(F32)
        unit, inv = norm_parts(mid[part, :])
        total = cotangent[part, :] + norm_back(unit, inv, upstream * gain[...])
        grad_mid[part, :] = total
        attn = total.astype(BF)
        grad_attn[part, :] = attn
        low = (dot_back(attn, proj_out[...]) * mask[part, :]).astype(BF)
        grad_low[part, :] = low
        value = (dot_back(attn, w_all[...]) + dot(low, in_all[...])).astype(BF)
        for d in range(count[1]):
            outs[d][part, :] = value[:, d * width : (d + 1) * width]

    repeat(2, one)


def message_body(count, pairs, me, up_in, down_out, proj_low, grad_attn, grad_low, *refs):
    attended = refs[: count * pairs]
    outs = refs[count * pairs : count * pairs + count]
    proj_out = refs[count * pairs + count]
    rank = up_in.shape[0]
    block = grad_low.shape[0]
    width = outs[0].shape[1]
    proj_out[...] = dot_over(proj_low[pl.ds(0, grad_low.shape[0]), :], grad_attn[...])
    for d in range(count):
        spot = place_of(0, d, count // 2) * block
        lanes = pl.ds(pl.multiple_of(owner_of(me[0], d, count) * width, width), width)
        outs[d][pl.ds(0, rank), :] = up_in[:, lanes].astype(BF)
        outs[d][pl.ds(rank, rank), :] = down_out[:, lanes].astype(BF)
        outs[d][pl.ds(2 * rank, rank), :] = proj_out[:, lanes].astype(BF)
        for p in range(pairs):
            outs[d][pl.ds(3 * rank, rank), p * PAIR : (p + 1) * PAIR] = dot_over(
                grad_low[...], attended[d * pairs + p][pl.ds(spot, block), :]
            ).astype(BF)


def pack_body(count, plain, pick, *refs):
    fixed = refs[:plain]
    messages = refs[plain : plain + count]
    out = refs[plain + count]
    rank = pick.shape[0]
    at = 0
    for ref in fixed:
        out[:, at : at + ref.shape[1]] = ref[...]
        at += ref.shape[1]
    width = messages[0].shape[1]
    for k in range(messages[0].shape[0] // rank):
        total = messages[0][pl.ds(k * rank, rank), :].astype(F32)
        for d in range(1, count):
            total = total + messages[d][pl.ds(k * rank, rank), :].astype(F32)
        out[:, at : at + width] = total.astype(BF)
        at += width
    out[:, at : at + pick.shape[1]] = pick[...]


def attend_back_body(pair, pairs, count, seq_len, *refs):
    first, last = pair == 0, pair == pairs - 1
    at = 0

    def take(number):
        nonlocal at
        at += number
        return refs[at - number : at]

    if last:
        (me,) = take(1)
    seq, kept = take(2)
    if first:
        pull_near, pull_far = take(2)
        grads = take(count)
    else:
        (grad_seq,) = take(1)
    if last:
        push, low_t, n1_near, n1_far, low_out = take(5)
        earlier = take(3 * (pairs - 1))
    grad_q, grad_k, grad_v = take(3)
    if last:
        part_t, qkv_out = take(2)
        messages = take(count)
    if first:
        grad_seq, grad_all = take(2)
    if last:
        part_seq, total_in = take(2)
    rows = seq.shape[0]
    width = seq.shape[1] // 3
    step = min(256, seq_len)
    scale = 1.0 / math.sqrt(HD)
    if first:
        block = grads[0].shape[0]
        near = pull_near.shape[1]
        for i in range(count):
            grad_all[pl.ds(i * block, block), :] = grads[i][...]
        grad_seq[...] = (
            dot(pull_near[...], grad_all[pl.ds(0, near), :])
            + dot(pull_far[...], grad_all[pl.ds(near, rows - near), :])
        ).astype(BF)
    if last:
        for p in range(pairs - 1):
            span = slice(p * PAIR, (p + 1) * PAIR)
            grad_q[span, :] = earlier[3 * p][...]
            grad_k[:, span] = earlier[3 * p + 1][...]
            grad_v[:, span] = earlier[3 * p + 2][...]
    base_row = pair * PAIR if last else 0

    def one_sequence(s):
        base = s * seq_len
        all_rows = rows_at(s, seq_len)
        lanes = pl.ds(pair * PAIR, PAIR)
        keys = seq[all_rows, pl.ds(width + pair * PAIR, PAIR)]
        values = seq[all_rows, pl.ds(2 * width + pair * PAIR, PAIR)]
        keys_t = keys.astype(F32).T.astype(BF)
        steps = seq_len // step
        sums_k = [None] * steps
        sums_v = [None] * steps
        for q in range(steps):
            span = pl.ds(pl.multiple_of(base + q * step, step), step)
            queries = seq[span, lanes]
            grad = grad_seq[span, lanes]
            seen = (q + 1) * step
            for h in range(2):
                own_q = head_lanes(queries, h)
                own_g = head_lanes(grad, h)
                probs = kept[s, h, :seen, q * step : (q + 1) * step]
                wide_probs = probs.astype(F32)
                mixed = wide_probs * dot_back(values[:seen], own_g)
                centre = jnp.sum(mixed, 0, keepdims=True)
                raw = (mixed - wide_probs * centre).astype(BF)
                grad_q[pl.ds(base_row + h * HD, HD), span] = (
                    dot(keys_t[h * HD : (h + 1) * HD, :seen], raw) * scale
                ).astype(BF)
                to_k = dot(raw, own_q)
                to_v = dot(probs, own_g)
                for b in range(q + 1):
                    cut = slice(b * step, (b + 1) * step)
                    sums_k[b] = to_k[cut] if sums_k[b] is None else sums_k[b] + to_k[cut]
                    sums_v[b] = to_v[cut] if sums_v[b] is None else sums_v[b] + to_v[cut]
        for b in range(steps):
            span = pl.ds(pl.multiple_of(base + b * step, step), step)
            grad_k[span, pl.ds(base_row, PAIR)] = sums_k[b].astype(BF)
            grad_v[span, pl.ds(base_row, PAIR)] = sums_v[b].astype(BF)

    repeat(rows // seq_len, one_sequence)
    if not last:
        return
    near = n1_near.shape[0]
    part = dot(low_out[0], grad_q[...]) + dot_back(low_out[1], grad_k[...]) + dot_back(low_out[2], grad_v[...])
    lane_at = lax.broadcasted_iota(jnp.int32, part.shape, 1) // seq_len
    rank_at = lax.broadcasted_iota(jnp.int32, part.shape, 0) // RANK
    part_seq[...] = jnp.where(lane_at == rank_at, part, 0.0).astype(BF)
    part_t[...] = dot_back(part_seq[...], push[...]).astype(BF)
    total_in[...] = dot(part_t[:, :near], n1_near[...]) + dot(part_t[:, near:], n1_far[...])
    qkv_out[:, :width] = dot_back(low_t[...], grad_q[...]).astype(BF)
    qkv_out[:, width : 2 * width] = dot(low_t[...], grad_k[...]).astype(BF)
    qkv_out[:, 2 * width :] = dot(low_t[...], grad_v[...]).astype(BF)
    for d in range(count):
        lanes = pl.ds(pl.multiple_of(owner_of(me[0], d, count) * width, width), width)
        messages[d][...] = total_in[:, lanes].astype(BF)


def qkv_back_body(ids, push, w_cat, low_in, grad_q, grad_k, grad_v, part_t, out, joined):
    block = out.shape[0] // len(ids)
    width = grad_k.shape[1]

    def one(i, at):
        rows = rows_at(i, block)
        place = push[rows_at(at, block), :]
        joined[:, :width] = dot_back(place, grad_q[...]).astype(BF)
        joined[:, width : 2 * width] = dot(place, grad_k[...]).astype(BF)
        joined[:, 2 * width :] = dot(place, grad_v[...]).astype(BF)
        low = dot_over(part_t[:, rows_at(at, block)], low_in[...])
        out[rows, :] = (dot_back(joined[...], w_cat[...]) + low).astype(BF)

    if ids == tuple(range(len(ids))):
        repeat(len(ids), lambda i: one(i, i))
    else:
        for i, at in enumerate(ids):
            one(i, at)


def add_pieces(total, pieces, i, half):
    part = rows_at(i, half)
    total = total + pieces[0][part, :].astype(F32) + pieces[1][part, :].astype(F32)
    halves = pieces[2:]
    number = len(halves) // 2
    for k in range(number):
        total = total + halves[i * number + k][...].astype(F32)
    return total


def input_back_body(tokens, grad_mid, gain, *refs):
    out, upstream = refs[-2:]
    half = tokens.shape[0] // 2
    for i in range(2):
        upstream[pl.ds(i * half, half), :] = add_pieces(0.0, refs[:-2], i, half)

    def one(i):
        part = rows_at(i, half)
        unit, inv = norm_parts(tokens[part, :].astype(F32))
        out[part, :] = grad_mid[part, :] + norm_back(unit, inv, upstream[part, :] * gain[...])

    repeat(2, one)


def result_body(mid, bias, *refs):
    out = refs[-1]
    half = out.shape[0] // 2
    for i in range(2):
        part = pl.ds(i * half, half)
        out[part, :] = add_pieces(mid[part, :] + bias[...], refs[:-1], i, half)


def spread_hidden_body(hid, found, up_out, down_in):
    pick = found[:, 2 * hid :]
    up_out[...] = dot_over(pick, found[:, :hid])
    down_in[...] = dot_over(found[:, hid : 2 * hid], pick)


def spread_wide_body(width, found, proj_in, wide):
    pick = found[:, 4 * width :]
    for k in range(3):
        wide[pl.ds(k * 128, 128), :] = dot_over(pick, found[:, k * width : (k + 1) * width]).astype(BF)
    proj_in[...] = dot_over(found[:, 3 * width : 4 * width], pick)


def spread_late_body(width, found, qkv_out, wide):
    pick = found[:, 4 * width :]
    for k in range(3):
        qkv_out[k] = dot_over(pick, found[:, k * width : (k + 1) * width])
    wide[...] = dot_over(pick, found[:, 3 * width : 4 * width]).astype(BF)


def place_wide_body(count, me, *refs):
    messages = refs[:count]
    up_in, down_out, proj_out = refs[count:]
    width = messages[0].shape[1]
    for d in range(count):
        span = pl.ds(pl.multiple_of(owner_of(me[0], d, count) * width, width), width)
        up_in[span, :] = messages[d][pl.ds(0, 128), :].astype(F32).T
        down_out[:, span] = messages[d][pl.ds(128, 128), :].astype(F32)
        proj_out[:, span] = messages[d][pl.ds(256, 128), :].astype(F32)


def place_late_body(count, me, *refs):
    messages = refs[:count]
    qkv_in = refs[count]
    width = messages[0].shape[1]
    for d in range(count):
        qkv_in[pl.ds(pl.multiple_of(owner_of(me[0], d, count) * width, width), width), :] = messages[d][...].astype(F32).T


def tie(value, *others):
    return lax.optimization_barrier((value, *others))[0]


def body(
    tensor_size,
    dp_size,
    tokens,
    cotangent,
    lengths,
    order,
    adapter_ids,
    norm1_gain,
    norm1_shift,
    qkv_weight,
    qv_bias,
    proj_weight,
    proj_bias,
    norm2_gain,
    norm2_shift,
    up_weight,
    up_bias,
    down_weight,
    down_bias,
    adapt_qkv_in,
    adapt_qkv_out,
    adapt_proj_in,
    adapt_proj_out,
    adapt_up_in,
    adapt_up_out,
    adapt_down_in,
    adapt_down_out,
):
    count = tensor_size
    chips = count // 2
    own, wide = tokens.shape
    width = qkv_weight.shape[2]
    pairs = width // PAIR
    hid = up_weight.shape[1]
    rows = order.shape[1]
    seqs = lengths.shape[1]
    seq_len = rows // seqs
    ranks = seqs * RANK
    near = 2 * own
    far = rows - near
    cols = adapt_qkv_in.shape[1]
    near_ids = (0, 1)
    even_ids = tuple(range(2, count, 2))
    odd_ids = tuple(range(3, count, 2))
    me = lax.axis_index("tensor")

    core_perm = [(t, t ^ 1) for t in range(count)]

    def core_swap(value):
        return lax.ppermute(value, "tensor", core_perm)

    def chip_hop(value, k):
        return lax.ppermute(value, "tensor", [(t, ((t // 2 + k) % chips) * 2 + t % 2) for t in range(count)])

    def hops_of(value):
        return [chip_hop(value, k) for k in range(1, chips)]

    def weave(value, swapped, moved):
        found = [value, swapped]
        for item in moved:
            found += [item, core_swap(item)]
        return found

    def exchange(messages):
        out = [messages[0], core_swap(messages[1])] + [None] * (count - 2)
        for k in range(1, chips):
            flat = [(t, ((t // 2 - k) % chips) * 2 + t % 2) for t in range(count)]
            cross = [(t, ((t // 2 - k) % chips) * 2 + (t % 2 ^ 1)) for t in range(count)]
            out[2 * (chips - k)] = lax.ppermute(messages[2 * k], "tensor", flat)
            out[2 * (chips - k) + 1] = lax.ppermute(messages[2 * k + 1], "tensor", cross)
        return out

    def join(left, right, name):
        return whole_call(add_body, [left, right], [shape(left.shape, BF)], name)[0]

    def send_far(joined):
        return [chip_hop(joined[(k - 1) * own : k * own] if chips > 2 else joined, -k) for k in range(1, chips)]

    def send_half(joined, part):
        half = own // 2
        return [
            chip_hop(joined[(k - 1) * own + part * half : (k - 1) * own + (part + 1) * half], -k)
            for k in range(1, chips)
        ]

    def dp_swap(value, stride):
        return lax.ppermute(value, "dp", [(i, i ^ stride) for i in range(dp_size)])

    def double(value, moved):
        return jnp.concatenate([value, moved], 0)

    def widen(value, stride):
        while stride:
            value = double(value, dp_swap(value, stride))
            stride //= 2
        return value

    place = me.reshape(1)
    dp_at = lax.axis_index("dp").reshape(1)
    weight_three = jnp.transpose(qkv_weight, (1, 0, 2))
    out_three = jnp.transpose(adapt_qkv_out, (1, 0, 2))
    row = lambda v: v.reshape(1, -1)

    top = dp_size // 2
    token_core = core_swap(tokens)
    token_hops = hops_of(tokens)
    grad_own = tie(cotangent, token_core).astype(BF)
    grad_core = core_swap(grad_own)

    prepared = whole_call(
        functools.partial(prep_body, seq_len, own, count),
        [order, proj_weight, adapt_qkv_in, out_three, adapt_proj_in, adapt_proj_out, adapt_up_in, adapt_up_out, adapt_down_in,
         adapt_down_out],
        [shape((ranks, wide), BF), shape((3, ranks, width), BF), shape((width + 16, wide), BF),
         shape((ranks, wide), BF), shape((ranks, wide), BF), shape((ranks, hid), BF),
         shape((ranks, hid), BF), shape((ranks, wide), BF), shape((rows, near), BF), shape((rows, far), BF),
         shape((rows, rows), BF), shape((rows, ranks), F32), shape((ranks, cols), BF), shape((1, rows), jnp.int32),
         shape((width // 2 + 16, wide), BF)],
        "prep",
        smem=[place, dp_at, lengths, adapter_ids],
        loose=tuple(range(10)),
        scratch=[pltpu.VMEM((rows, 1), jnp.int32)],
    )
    c_qkv_in, c_qkv_out, proj_own, c_proj_out, c_up_in, c_up_out, c_down_in, c_down_out = prepared[:8]
    pull_near, pull_far, push, mask, pick, limit, proj_half = prepared[8:]
    proj_core = core_swap(proj_own)
    proj_hops = hops_of(proj_half)

    norm1 = [row(norm1_gain), row(norm1_shift), weight_three, qv_bias, c_qkv_in, c_qkv_out]
    n1_near, low1_near, moved_near = whole_call(
        functools.partial(qkv_body, near_ids, False),
        [mask] + norm1 + [pull_near, tokens, token_core],
        [shape((near, wide), BF), shape((near, ranks), BF), shape((rows, 3 * width), F32)],
        "qkv_near",
        loose=(1, 2, 3, 4, 8, 9),
        long=True,
        scratch=[pltpu.VMEM((near, 3 * width), BF), pltpu.VMEM((near, wide), BF), pltpu.VMEM((near, ranks), F32)],
    )
    token_hops = [tie(item, low1_near) for item in token_hops]
    token_blocks = weave(tokens, token_core, token_hops)
    n1_far, low1_far, qkv_seq = whole_call(
        functools.partial(qkv_body, tuple(range(2, count)), True),
        [mask] + norm1 + [pull_far] + token_blocks[2:] + [moved_near],
        [shape((far, wide), BF), shape((far, ranks), BF), shape((rows, 3 * width), BF)],
        "qkv_far",
        scratch=[pltpu.VMEM((far, 3 * width), BF), pltpu.VMEM((far, wide), BF), pltpu.VMEM((far, ranks), F32)],
    )

    grad_hops = hops_of(tie(grad_own, low1_far))
    sums = []
    attended = []
    seq_in = qkv_seq
    for pair in range(pairs):
        part, kept = whole_call(
            functools.partial(attend_body, seq_len, pair),
            [limit, seq_in, push],
            [shape((rows, PAIR), BF), shape((seqs, 2, seq_len, seq_len), BF)],
            f"attend{pair}",
            scratch=[pltpu.VMEM((PAIR, rows), BF)],
        )
        sums.append(kept)
        attended.append(part)
        if pair == 0:
            seq_in = tie(qkv_seq, part)
    after = attended[-1]
    gathered_heads = []
    for part in attended:
        gathered_heads.append(weave(part, core_swap(part), hops_of(part)))
    heads = [gathered_heads[p][d] for d in range(count) for p in range(pairs)]

    proj_parts = []
    for item in proj_hops:
        item = tie(item, after)
        other = dp_swap(item[: width // 2], 1)
        proj_parts += [item, other, core_swap(item), core_swap(other)]
    grad_blocks = weave(grad_own, grad_core, [tie(item, after) for item in grad_hops])
    w_all, in_all, w_cat, low_t = whole_call(
        functools.partial(join_body, count),
        [low1_near, low1_far, push, weight_three, proj_own, proj_core] + proj_parts,
        [shape((wide, wide), BF), shape((ranks, wide), BF), shape((wide, 3 * width), BF), shape((ranks, rows), BF)],
        "join",
        smem=[dp_at],
    )

    def block_call(ids, gate, name):
        size = len(ids) * own
        extra = [shape((size, ranks), BF), shape((size, wide), F32)] if 0 in ids else []
        keep = mask if gate is None else tie(mask, gate)
        return whole_call(
            functools.partial(block_body, ids, count, pairs, min(512, hid)),
            [keep, w_all, in_all, c_proj_out, row(proj_bias), row(norm2_gain), row(norm2_shift), c_up_in, up_weight,
             row(up_bias), c_up_out, down_weight, c_down_in, c_down_out]
            + [token_blocks[i] for i in ids] + [grad_blocks[i] for i in ids] + heads,
            [shape((size, wide), BF), shape((size, wide), BF), shape((size, ranks), BF), shape((size, ranks), BF),
             shape((size, ranks), BF), shape((size, hid), BF), shape((size, hid), BF), shape((size, ranks), BF)]
            + extra,
            name,
            scratch=[pltpu.VMEM((size, wide), BF)] * 3
            + [pltpu.VMEM((size, ranks), F32), pltpu.VMEM((own, wide), F32)] + [pltpu.VMEM((own, ranks), F32)] * 2,
            long=gate is not None,
        )

    odd = block_call(odd_ids, None, "block_odd")
    odd_moved = core_swap(odd[0])
    even = block_call(even_ids, odd[3], "block_even")
    up_joined = join(even[0], odd_moved, "up_join")
    up_hops = send_far(up_joined)
    mine = block_call(near_ids, up_joined, "block_near")
    up_swap = core_swap(mine[0][own:])
    groups = (mine, even, odd)
    order_ids = (near_ids, even_ids, odd_ids)
    pack_hidden, p_up_in, p_down_out = whole_call(
        functools.partial(hidden_grads_body, 3, tuple(len(i) for i in order_ids)),
        [pick] + [g[k] for k in (2, 6, 4, 5, 3, 1, 7) for g in groups]
        + [grad_blocks[i] for ids in order_ids for i in ids],
        [shape((ranks, 2 * hid + cols), BF), shape((ranks, wide), F32), shape((ranks, wide), F32)],
        "hidden_grads",
    )
    up_hops = [tie(item, p_up_in) for item in up_hops]
    proj_low, mid = mine[8:]
    back = whole_call(
        functools.partial(mid_back_body, (2 + len(up_hops), count)),
        [mask, cotangent, mid, row(norm2_gain), c_proj_out, w_all, in_all, mine[0], up_swap] + up_hops,
        [shape((own, wide), F32), shape((own, wide), BF), shape((own, ranks), BF)]
        + [shape((own, width), BF)] * count,
        "mid_back",
        long=True,
    )
    grad_mid, grad_attn, grad_proj_low = back[:3]
    grad_att = exchange(back[3:])
    hidden_moved = dp_swap(tie(pack_hidden, grad_proj_low), top)

    messages = whole_call(
        functools.partial(message_body, count, pairs),
        [p_up_in, p_down_out, proj_low, grad_attn, grad_proj_low] + heads,
        [shape((4 * ranks, width), BF)] * count,
        "message",
        smem=[place],
        scratch=[pltpu.VMEM((ranks, wide), F32)],
        long=True,
    )
    down_parts = whole_call(
        functools.partial(down_body, 3, own),
        [tie(down_weight, messages[0]), c_down_out] + [g[5] for g in groups] + [g[7] for g in groups],
        [shape(g[0].shape, BF) for g in groups],
        "down",
        long=True,
    )
    down_mine, down_even, down_odd = down_parts
    grad_att = [grad_att[0]] + [tie(item, down_mine) for item in grad_att[1:]]
    wide_messages = exchange([tie(item, *grad_att[1:]) for item in messages])
    down_moved = core_swap(tie(down_odd, *grad_att[1:]))
    down_swap = core_swap(tie(down_mine[own:], *grad_att[1:]))

    back_pieces = []
    grad_seq = None
    for pair in range(pairs):
        last = pair == pairs - 1
        inputs = [qkv_seq, sums[pair]]
        outs = [shape((PAIR, rows), BF), shape((rows, PAIR), BF), shape((rows, PAIR), BF)]
        scratch = []
        if pair == 0:
            inputs += [pull_near, pull_far] + grad_att
        else:
            inputs += [grad_seq]
        if last:
            inputs += [push, low_t, n1_near, n1_far, c_qkv_out] + back_pieces
            outs = [shape((width, rows), BF), shape((rows, width), BF), shape((rows, width), BF),
                    shape((ranks, rows), BF), shape((ranks, 3 * width), BF)] + [shape((ranks, width), BF)] * count
        if pair == 0:
            if last:
                scratch += [pltpu.VMEM((rows, width), BF)]
            else:
                outs += [shape((rows, width), BF)]
            scratch += [pltpu.VMEM((rows, width), BF)]
        if last:
            scratch += [pltpu.VMEM((ranks, rows), BF), pltpu.VMEM((ranks, wide), F32)]
        results = whole_call(
            functools.partial(attend_back_body, pair, pairs, count, seq_len),
            inputs,
            outs,
            f"attend_back{pair}",
            smem=[place] if last else [],
            scratch=scratch,
            long=True,
        )
        if pair == 0:
            passed = results[0]
            wide_messages = [wide_messages[0]] + [tie(item, passed) for item in wide_messages[1:]]
            (pack_wide,) = whole_call(
                functools.partial(pack_body, count, 0),
                [pick] + wide_messages,
                [shape((ranks, 4 * width + cols), BF)],
                "pack_wide",
            )
            hidden_half = double(pack_hidden, tie(hidden_moved, passed, *wide_messages))
            hidden_moved = dp_swap(hidden_half, top // 2)
            hidden_first = dp_swap(hidden_half, top // 4)
            wide_moved = dp_swap(pack_wide, top)
            down_joined = join(down_even, tie(down_moved, passed, *wide_messages), "down_join")
            down_first = send_half(down_joined, 0)
        if not last:
            back_pieces += list(results[:3])
            grad_seq = tie(results[3], pack_wide, hidden_half, down_joined)
    grad_q, grad_k, grad_v, part_t, g_qkv_out = results[:5]
    down_first = [tie(item, part_t) for item in down_first]
    hidden_moved = tie(hidden_moved, part_t)
    hidden_first = tie(hidden_first, part_t)
    late_messages = exchange(results[5:])
    hidden_second = dp_swap(hidden_moved, top // 4)
    wide_moved_first = tie(wide_moved, part_t)
    wide_found = double(pack_wide, wide_moved_first)
    wide_moved = dp_swap(wide_found, top // 2)

    def unproject(ids, gates, name):
        size = len(ids) * own
        return whole_call(
            functools.partial(qkv_back_body, ids),
            [push, w_cat, c_qkv_in, grad_q, grad_k, grad_v, tie(part_t, *gates)],
            [shape((size, wide), BF)],
            name,
            scratch=[pltpu.VMEM((own, 3 * width), BF)],
            long=True,
        )[0]

    odd_part = unproject(odd_ids, [wide_moved_first, hidden_moved, hidden_first, *down_first], "qkv_back_odd")
    odd_moved = core_swap(odd_part)
    even_part = unproject(even_ids, [odd_part], "qkv_back_even")
    qkv_joined = join(even_part, tie(odd_moved, *late_messages[1:], wide_moved), "qkv_join")
    qkv_first = send_half(qkv_joined, 0)
    late_messages = [late_messages[0]] + [tie(item, qkv_joined) for item in late_messages[1:]]
    (pack_late,) = whole_call(
        functools.partial(pack_body, count, 1),
        [pick, g_qkv_out] + late_messages,
        [shape((ranks, 4 * width + cols), BF)],
        "pack_late",
    )
    late_moved = dp_swap(pack_late, top)
    wide_found = double(wide_found, wide_moved)
    wide_moved = dp_swap(wide_found, top // 4)
    near_part = unproject(near_ids, [qkv_joined, pack_late, hidden_second], "qkv_back_near")
    qkv_swap = core_swap(near_part[own:])
    qkv_first = [tie(item, near_part) for item in qkv_first]
    qkv_second = send_half(tie(qkv_joined, *qkv_first), 1)
    late_found = double(pack_late, tie(late_moved, near_part, *qkv_first))
    late_moved = dp_swap(late_found, top // 2)
    late_moved = tie(late_moved, *qkv_second)
    wide_found = widen(double(wide_found, tie(wide_moved, late_moved)), top // 8)
    proj_in_full, wide_part = whole_call(
        functools.partial(spread_wide_body, width),
        [wide_found],
        [shape((width, cols), F32), shape((3 * cols, width), BF)],
        "spread_wide",
        final=(0,),
    )
    wide_blocks = weave(wide_part, core_swap(wide_part), hops_of(wide_part))
    late_found = double(late_found, late_moved)
    late_moved = dp_swap(late_found, top // 4)
    down_second = send_half(tie(down_joined, *qkv_second), 1)
    (grad_input,) = whole_call(
        input_back_body,
        [tokens, grad_mid, row(norm1_gain), near_part, qkv_swap, *qkv_first, *qkv_second],
        [shape((own, wide), F32)],
        "input_back",
        scratch=[pltpu.VMEM((own, wide), F32)],
        final=(0,),
    )
    up_in_full, down_out_full, proj_out_full = whole_call(
        functools.partial(place_wide_body, count),
        [tie(wide_blocks[0], grad_input)] + wide_blocks[1:],
        [shape((wide, cols), F32), shape((cols, wide), F32), shape((cols, wide), F32)],
        "place_wide",
        smem=[place],
        final=(0, 1, 2),
    )
    late_found = widen(double(late_found, tie(late_moved, grad_input)), top // 8)
    qkv_out_full, late_part = whole_call(
        functools.partial(spread_late_body, width),
        [late_found],
        [shape((3, cols, width), F32), shape((cols, width), BF)],
        "spread_late",
        final=(0,),
    )
    late_blocks = weave(late_part, core_swap(late_part), hops_of(late_part))
    (result,) = whole_call(
        result_body,
        [mid, row(down_bias), down_mine, down_swap, *down_first, *[tie(item, late_part) for item in down_second]],
        [shape((own, wide), F32)],
        "result",
        final=(0,),
    )
    hidden_found = jnp.concatenate([hidden_half, hidden_moved, hidden_first, tie(hidden_second, result)], 0)
    up_out_full, down_in_full = whole_call(
        functools.partial(spread_hidden_body, hid),
        [widen(hidden_found, top // 8)],
        [shape((cols, hid), F32), shape((hid, cols), F32)],
        "spread_hidden",
        final=(0, 1),
    )
    (qkv_in_full,) = whole_call(
        functools.partial(place_late_body, count),
        [late_blocks[0]] + [tie(item, up_out_full) for item in late_blocks[1:]],
        [shape((wide, cols), F32)],
        "place_late",
        smem=[place],
        final=(0,),
    )
    return (
        result,
        grad_input,
        qkv_in_full,
        jnp.transpose(qkv_out_full, (1, 0, 2)),
        proj_in_full,
        proj_out_full,
        up_in_full,
        up_out_full,
        down_in_full,
        down_out_full,
    )


def solution(mesh):
    in_specs = (
        P(("dp", "tensor"), None),
        P(("dp", "tensor"), None),
        P("dp", None),
        P("dp", None),
        P("dp", None),
        P(),
        P(),
        P(None, None, "tensor"),
        P(None, "tensor"),
        P("tensor", None),
        P(),
        P(),
        P(),
        P(None, "tensor"),
        P("tensor"),
        P("tensor", None),
        P(),
        P(),
        P(None, None, "tensor"),
        P("tensor", None),
        P(),
        P(),
        P(None, "tensor"),
        P("tensor", None),
        P(),
    )
    out_specs = (
        P(("dp", "tensor"), None),
        P(("dp", "tensor"), None),
        P(),
        P(None, None, "tensor"),
        P("tensor", None),
        P(),
        P(),
        P(None, "tensor"),
        P("tensor", None),
        P(),
    )
    run = functools.partial(body, mesh.shape["tensor"], mesh.shape["dp"])
    return jax.shard_map(run, mesh=mesh, in_specs=in_specs, out_specs=out_specs, check_vma=False)
```

profile of v0, /device:TPU:0, one launch (start us, length us, event | category | flops | bytes accessed | tf_op | source)
XLA Modules:
  0.0 153.7 jit_solution(12767275916369019250)
XLA Ops:
  1.2 2.6 %collective-permute-start.1 = (bf16[256,1024]{1,0:T(8,128)(2,1)}, bf16[256,1024]{1,0:T(8,128)(2,1)S(1)}, u32[]{:S(2)}, u32[]{:S(2)}) collective-permute-start(bf16[256,1024]{1,0:T(8,128)(2,1)} %tokens.1), channel_id=1, source_target_pairs={{0,2},{1,3},{2,0},{3,1},{4,6},{5,7},{6,4},{7,5},{8,10},{9,11},{10,... | collective-permute-start | bytes 1572872 | tf_op jit(solution)/shard_map/ppermute | solution.py:689
  5.0 3.9 %prep.1 = (bf16[32,1024]{1,0:T(8,128)(2,1)S(1)}, bf16[3,32,256]{2,1,0:T(8,128)(2,1)S(1)}, bf16[272,1024]{1,0:T(8,128)(2,1)S(1)}, bf16[32,1024]{1,0:T(8,128)(2,1)...) custom-call(s32[1]{0:T(128)} %bitcast.me.refs_0_, ...), custom_call_target="tpu_custom_call" | custom-call | tf_op jit(solution)/shard_map/prep/pallas_call | solution.py:46
  9.8 6.2 %qkv_near.1 = (bf16[512,1024]{1,0:T(8,128)(2,1)S(1)}, bf16[512,32]{1,0:T(8,128)(2,1)S(1)}, f32[1024,768]{1,0:T(8,128)S(1)}) custom-call(f32[1024,32]{1,0:T(8,128)S(1)} %get-tuple-element.186.mask, f32[1,1024]{1,0:T(1,128)} %bitcast.28, f32[1,1024]{1,0:T(1,128)} %bitcast.31, bf16[3,1024,256]{2,1,0:T(8,128)(2,1)} %bitcast.12, f32[2,256]{1,0:T(2,128)} %bias.3, ...), custom_call_target="tpu_custom_call" | custom-call | tf_op jit(solution)/shard_map/qkv_near/pallas_call | solution.py:46
  16.5 1.8 %collective-permute-start.4 = (bf16[144,1024]{1,0:T(8,128)(2,1)S(1)}, bf16[144,1024]{1,0:T(8,128)(2,1)S(1)}, u32[]{:S(2)}, u32[]{:S(2)}) collective-permute-start(bf16[144,1024]{1,0:T(8,128)(2,1)S(1)} %get-tuple-element.165), channel_id=1, source_target_pairs={{0,2},{1,3},{2,0},{3,1},{4,6},{5,7},{6,4},{7,5},{8,10},{9,11},{10,... | collective-permute-start | bytes 884744 | tf_op jit(solution)/shard_map/ppermute | solution.py:689
  18.6 4.4 %qkv_far.1 = (bf16[512,1024]{1,0:T(8,128)(2,1)S(1)}, bf16[512,32]{1,0:T(8,128)(2,1)S(1)}, bf16[1024,768]{1,0:T(8,128)(2,1)S(1)}) custom-call(f32[1024,32]{1,0:T(8,128)S(1)} %get-tuple-element.186.mask, f32[1,1024]{1,0:T(1,128)S(1)} %bitcast.29, f32[1,1024]{1,0:T(1,128)S(1)} %bitcast.32, bf16[3,1024,256]{2,1,0:T(8,128)(2,1)S(1)} %bitcast.13, ...), custom_call_target="tpu_custom_call" | custom-call | tf_op jit(solution)/shard_map/qkv_far/pallas_call | solution.py:46
  24.6 4.4 %attend0.1 = (bf16[1024,128]{1,0:T(8,128)(2,1)S(1)}, bf16[2,2,512,512]{3,2,1,0:T(8,128)(2,1)S(1)}) custom-call(s32[1,1024]{1,0:T(1,128)S(1)} %get-tuple-element.166.limit, bf16[1024,768]{1,0:T(8,128)(2,1)S(1)} %get-tuple-element.169.seq.refs_0_.refs_1_, bf16[1024,1024]{1,0:T(8,128)(2,1)S(1)} %get-tuple-element.163.push.refs_4_), custom_call_target="tpu_custom_call" | custom-call | tf_op jit(solution)/shard_map/attend0/pallas_call | solution.py:46
  29.0 4.4 %attend1.1 = (bf16[1024,128]{1,0:T(8,128)(2,1)S(1)}, bf16[2,2,512,512]{3,2,1,0:T(8,128)(2,1)S(1)}) custom-call(s32[1,1024]{1,0:T(1,128)S(1)} %get-tuple-element.166.limit, bf16[1024,768]{1,0:T(8,128)(2,1)S(1)} %get-tuple-element.169.seq.refs_0_.refs_1_, bf16[1024,1024]{1,0:T(8,128)(2,1)S(1)} %get-tuple-element.163.push.refs_4_), custom_call_target="tpu_custom_call" | custom-call | tf_op jit(solution)/shard_map/attend1/pallas_call | solution.py:46
  35.6 6.0 %collective-permute-done.5.refs_3_ = bf16[128,1024]{1,0:T(8,128)(2,1)S(1)} collective-permute-done((bf16[128,1024]{1,0:T(8,128)(2,1)S(1)}, bf16[128,1024]{1,0:T(8,128)(2,1)S(1)}, u32[]{:S(2)}, u32[]{:S(2)}) %collective-permute-start.5) | collective-permute-done | bytes 262176 | tf_op jit(solution)/shard_map/ppermute | solution.py:723
  44.2 5.2 %collective-permute-done.13.refs_7_.refs_9_.refs_5_ = bf16[1024,128]{1,0:T(8,128)(2,1)S(1)} collective-permute-done((bf16[1024,128]{1,0:T(8,128)(2,1)S(1)}, bf16[1024,128]{1,0:T(8,128)(2,1)S(1)}, u32[]{:S(2)}, u32[]{:S(2)}) %collective-permute-start.13) | collective-permute-done | bytes 262176 | tf_op jit(solution)/shard_map/ppermute | solution.py:689
  52.2 5.2 %block_odd.1 = (bf16[256,1024]{1,0:T(8,128)(2,1)S(1)}, bf16[256,1024]{1,0:T(8,128)(2,1)S(1)}, bf16[256,32]{1,0:T(8,128)(2,1)S(1)}, bf16[256,32]{1,0:T(8,128)(2,1...) custom-call(f32[1024,32]{1,0:T(8,128)S(1)} %get-tuple-element.186.ma, ...), custom_call_target="tpu_custom_call" | custom-call | tf_op jit(solution)/shard_map/block_odd/pallas_call | solution.py:46
  58.1 5.1 %block_even.1 = (bf16[256,1024]{1,0:T(8,128)(2,1)S(1)}, bf16[256,1024]{1,0:T(8,128)(2,1)S(1)}, bf16[256,32]{1,0:T(8,128)(2,1)S(1)}, bf16[256,32]{1,0:T(8,128)(2,...) custom-call(f32[1024,32]{1,0:T(8,128)S(1)} %get-tuple-element.186.ma, ...), custom_call_target="tpu_custom_call" | custom-call | tf_op jit(solution)/shard_map/block_even/pallas_call | solution.py:46
  64.3 10.5 %block_near.1 = (bf16[512,1024]{1,0:T(8,128)(2,1)S(1)}, bf16[512,1024]{1,0:T(8,128)(2,1)S(1)}, bf16[512,32]{1,0:T(8,128)(2,1)S(1)}, bf16[512,32]{1,0:T(8,128)(2,...) custom-call(f32[1024,32]{1,0:T(8,128)S(1)} %get-tuple-element.186.ma, ...), custom_call_target="tpu_custom_call" | custom-call | tf_op jit(solution)/shard_map/block_near/pallas_call | solution.py:46
  77.6 2.9 %mid_back.1 = (f32[256,1024]{1,0:T(8,128)S(1)}, bf16[256,1024]{1,0:T(8,128)(2,1)S(1)}, bf16[256,32]{1,0:T(8,128)(2,1)S(1)}, bf16[256,256]{1,0:T(8,128)(2,1)S(1)}...) custom-call(f32[1024,32]{1,0:T(8,128)S(1)} %get-tuple-element.186.mask, ...), custom_call_target="tpu_custom_call" | custom-call | tf_op jit(solution)/shard_map/mid_back/pallas_call | solution.py:46
  82.9 3.1 %down.1 = (bf16[512,1024]{1,0:T(8,128)(2,1)S(1)}, bf16[256,1024]{1,0:T(8,128)(2,1)S(1)}, bf16[256,1024]{1,0:T(8,128)(2,1)S(1)}) custom-call(bf16[1024,1024]{1,0:T(8,128)(2,1)S(1)} %copy-done, bf16[32,1024]{1,0:T(8,128)(2,1)S(1)} %get-tuple-element.178.down_out, bf16[512,1024]{1,0:T(8,128)(2,1)S(1)} %get-tuple-element.198.refs_9_.refs_0_, ...), custom_call_target="tpu_custom_call" | custom-call | tf_op jit(solution)/shard_map/down/pallas_call | solution.py:46
  86.0 2.7 %collective-permute-start.29 = (bf16[32,2176]{1,0:T(8,128)(2,1)S(1)}, bf16[32,2176]{1,0:T(8,128)(2,1)S(1)}, u32[]{:S(2)}, u32[]{:S(2)}) collective-permute-start(bf16[32,2176]{1,0:T(8,128)(2,1)S(1)} %get-tuple-element.246), channel_id=1, source_target_pairs={{0,16},{4,20},{8,24},{12,28},{16,0},{20,4},{24,8},{28,12},{1,17},{... | collective-permute-start | bytes 417800 | tf_op jit(solution)/shard_map/ppermute | solution.py:723
  91.4 4.7 %attend_back0.1 = (bf16[128,1024]{1,0:T(8,128)(2,1)S(1)}, bf16[1024,128]{1,0:T(8,128)(2,1)S(1)}, bf16[1024,128]{1,0:T(8,128)(2,1)S(1)}, bf16[1024,256]{1,0:T(8,128)(2,1)S(1)}) custom-call(bf16[1024,768]{1,0:T(8,128)(2,1)S(1)} %get-tuple-element.169.seq.refs_0_.refs_1_, bf16[2,2,512,512]{3,2,1,0:T(8,128)(2,1)S(1)} %get-tuple-element.229.refs_1_, ...), custom_call_target="tpu_custom_call" | custom-call | tf_op jit(solution)/shard_map/attend_back0/pallas_call | solution.py:46
  100.2 2.6 %collective-permute-start.30 = (bf16[32,1152]{1,0:T(8,128)(2,1)S(1)}, bf16[32,1152]{1,0:T(8,128)(2,1)S(1)}, u32[]{:S(2)}, u32[]{:S(2)}) collective-permute-start(bf16[32,1152]{1,0:T(8,128)(2,1)S(1)} %pack_wide.1), channel_id=1, source_target_pairs={{0,16},{4,20},{8,24},{12,28},{16,0},{20,4},{24,8},{28,12},{1,17},{... | collective-permute-start | bytes 221192 | tf_op jit(solution)/shard_map/ppermute | solution.py:723
  102.9 5.7 %attend_back1.1 = (bf16[256,1024]{1,0:T(8,128)(2,1)S(1)}, bf16[1024,256]{1,0:T(8,128)(2,1)S(1)}, bf16[1024,256]{1,0:T(8,128)(2,1)S(1)}, bf16[32,1024]{1,0:T(8,12...) custom-call(s32[1]{0:T(128)} %bitcast.me.refs_0_, ...), custom_call_target="tpu_custom_call" | custom-call | tf_op jit(solution)/shard_map/attend_back1/pallas_call | solution.py:46
  108.6 1.7 %qkv_back_odd.1 = bf16[256,1024]{1,0:T(8,128)(2,1)S(1)} custom-call(bf16[1024,1024]{1,0:T(8,128)(2,1)S(1)} %get-tuple-element.163.push.refs_4_, bf16[1024,768]{1,0:T(8,128)(2,1)S(1)} %get-tuple-element.256.w_cat, bf16[32,1024]{1,0:T(8,128)(2,1)S(1)} %get-tuple-element.155.low_in, bf16[256,1024]{1,0:T(8,128)(2,1)S(1)} %get-tuple-element.257.grad_q, ...), custom_call_target="tpu_custom_call" | custom-call | tf_op jit(solution)/shard_map/qkv_back_odd/pallas_call | solution.py:46
  119.3 3.1 %collective-permute-done.39 = bf16[64,2176]{1,0:T(8,128)(2,1)S(1)} collective-permute-done((bf16[64,2176]{1,0:T(8,128)(2,1)S(1)}, bf16[64,2176]{1,0:T(8,128)(2,1)S(1)}, u32[]{:S(2)}, u32[]{:S(2)}) %collective-permute-start.39) | collective-permute-done | bytes 278560 | tf_op jit(solution)/shard_map/ppermute | solution.py:723
  122.4 3.5 %qkv_back_near.1.refs_0_ = bf16[512,1024]{1,0:T(8,128)(2,1)S(1)} custom-call(bf16[1024,1024]{1,0:T(8,128)(2,1)S(1)} %get-tuple-element.163.push.refs_4_, bf16[1024,768]{1,0:T(8,128)(2,1)S(1)} %get-tuple-element.256.w_cat, bf16[32,1024]{1,0:T(8,128)(2,1)S(1)} %get-tuple-element.155.low_in, bf16[256,1024]{1,0:T(8,128)(2,1)S(1)} %get-tuple-element.257.grad_q, ...), custom_call_target="tpu_custom_call" | custom-call | tf_op jit(solution)/shard_map/qkv_back_near/pallas_call | solution.py:46
  129.3 3.3 %collective-permute-done.43 = bf16[64,1152]{1,0:T(8,128)(2,1)S(1)} collective-permute-done((bf16[64,1152]{1,0:T(8,128)(2,1)S(1)}, bf16[64,1152]{1,0:T(8,128)(2,1)S(1)}, u32[]{:S(2)}, u32[]{:S(2)}) %collective-permute-start.43) | collective-permute-done | bytes 147488 | tf_op jit(solution)/shard_map/ppermute | solution.py:723
  139.7 1.9 %input_back.1 = f32[256,1024]{1,0:T(8,128)} custom-call(bf16[256,1024]{1,0:T(8,128)(2,1)S(1)} %copy-done.3, f32[256,1024]{1,0:T(8,128)S(1)} %get-tuple-element.280.grad_mid, f32[1,1024]{1,0:T(1,128)S(1)} %bitcast.30, bf16[512,1024]{1,0:T(8,128)(2,1)S(1)} %qkv_back_near.1.refs_0_, bf16[256,1024]{1,0:T(8,128)(2,1)S(1)} %collective-permute-done.45.refs_1_, ...), custom_call_target="tpu_custom_call" | custom-call | tf_op jit(solution)/shard_map/input_back/pallas_call | solution.py:46
  145.3 3.1 %collective-permute-done.41.refs_3_ = bf16[128,1024]{1,0:T(8,128)(2,1)S(1)} collective-permute-done((bf16[128,1024]{1,0:T(8,128)(2,1)S(1)}, bf16[128,1024]{1,0:T(8,128)(2,1)S(1)}, u32[]{:S(2)}, u32[]{:S(2)}) %collective-permute-start.41) | collective-permute-done | bytes 262176 | tf_op jit(solution)/shard_map/ppermute | solution.py:689
  (166 shorter events, 54.4 us)
Async XLA Ops:
  0.6 8.3 %collective-permute-start = (bf16[256,1024]{1,0:T(8,128)(2,1)}, bf16[256,1024]{1,0:T(8,128)(2,1)S(1)}, u32[]{:S(2)}, u32[]{:S(2)}) collective-permute-start(bf16[256,1024]{1,0:T(8,128)(2,1)} %tokens.1), channel_id=1, source_target_pairs={{0,1},{1,0},{2,3},{3,2},{4,5},{5,4},{6,7},{7,6},{8,9},{9,8},{10,11... | collective-permute-start | bytes 1572872 | tf_op jit(solution)/shard_map/ppermute | solution.py:686
  1.2 15.3 %collective-permute-start.1 = (bf16[256,1024]{1,0:T(8,128)(2,1)}, bf16[256,1024]{1,0:T(8,128)(2,1)S(1)}, u32[]{:S(2)}, u32[]{:S(2)}) collective-permute-start(bf16[256,1024]{1,0:T(8,128)(2,1)} %tokens.1), channel_id=1, source_target_pairs={{0,2},{1,3},{2,0},{3,1},{4,6},{5,7},{6,4},{7,5},{8,10},{9,11},{10,... | collective-permute-start | bytes 1572872 | tf_op jit(solution)/shard_map/ppermute | solution.py:689
  16.5 17.0 %collective-permute-start.4 = (bf16[144,1024]{1,0:T(8,128)(2,1)S(1)}, bf16[144,1024]{1,0:T(8,128)(2,1)S(1)}, u32[]{:S(2)}, u32[]{:S(2)}) collective-permute-start(bf16[144,1024]{1,0:T(8,128)(2,1)S(1)} %get-tuple-element.165), channel_id=1, source_target_pairs={{0,2},{1,3},{2,0},{3,1},{4,6},{5,7},{6,4},{7,5},{8,10},{9,11},{10,... | collective-permute-start | bytes 884744 | tf_op jit(solution)/shard_map/ppermute | solution.py:689
  18.2 24.0 %collective-permute-start.3 = (bf16[272,1024]{1,0:T(8,128)(2,1)S(1)}, bf16[272,1024]{1,0:T(8,128)(2,1)S(1)}, u32[]{:S(2)}, u32[]{:S(2)}) collective-permute-start(bf16[272,1024]{1,0:T(8,128)(2,1)S(1)} %get-tuple-element.164.refs_0_), channel_id=1, source_target_pairs={{0,1},{1,0},{2,3},{3,2},{4,5},{5,4},{6,7},{7,6},{8,9},{9,8},{10,11... | collective-permute-start | bytes 1671176 | tf_op jit(solution)/shard_map/ppermute | solution.py:686
  23.0 19.3 %collective-permute-start.8 = (bf16[256,1024]{1,0:T(8,128)(2,1)S(1)}, bf16[256,1024]{1,0:T(8,128)(2,1)S(1)}, u32[]{:S(2)}, u32[]{:S(2)}) collective-permute-start(bf16[256,1024]{1,0:T(8,128)(2,1)S(1)} %convert_element_type.3.refs_2_.refs_21_), channel_id=1, source_target_pairs={{0,2},{1,3},{2,0},{3,1},{4,6},{5,7},{6,4},{7,5},{8,10},{9,11},{10,... | collective-permute-start | bytes 1572872 | tf_op jit(solution)/shard_map/ppermute | solution.py:689
  33.5 8.1 %collective-permute-start.5 = (bf16[128,1024]{1,0:T(8,128)(2,1)S(1)}, bf16[128,1024]{1,0:T(8,128)(2,1)S(1)}, u32[]{:S(2)}, u32[]{:S(2)}) collective-permute-start(bf16[128,1024]{1,0:T(8,128)(2,1)S(1)} %slice.24), channel_id=1, source_target_pairs={{0,4},{4,0},{8,12},{12,8},{16,20},{20,16},{24,28},{28,24},{1,5},{5... | collective-permute-start | bytes 786440 | tf_op jit(solution)/shard_map/ppermute | solution.py:723
  35.1 14.3 %collective-permute-start.6 = (bf16[144,1024]{1,0:T(8,128)(2,1)S(1)}, bf16[144,1024]{1,0:T(8,128)(2,1)S(1)}, u32[]{:S(2)}, u32[]{:S(2)}) collective-permute-start(bf16[144,1024]{1,0:T(8,128)(2,1)S(1)} %collective-permute-done.4.refs_2_), channel_id=1, source_target_pairs={{0,1},{1,0},{2,3},{3,2},{4,5},{5,4},{6,7},{7,6},{8,9},{9,8},{10,11... | collective-permute-start | bytes 884744 | tf_op jit(solution)/shard_map/ppermute | solution.py:686
  35.1 9.1 %collective-permute-start.12 = (bf16[1024,128]{1,0:T(8,128)(2,1)S(1)}, bf16[1024,128]{1,0:T(8,128)(2,1)S(1)}, u32[]{:S(2)}, u32[]{:S(2)}) collective-permute-start(bf16[1024,128]{1,0:T(8,128)(2,1)S(1)} %get-tuple-element.168.refs_2_.refs_4_.refs_0_), channel_id=1, source_target_pairs={{0,2},{1,3},{2,0},{3,1},{4,6},{5,7},{6,4},{7,5},{8,10},{9,11},{10,... | collective-permute-start | bytes 786440 | tf_op jit(solution)/shard_map/ppermute | solution.py:689
  42.3 9.5 %collective-permute-start.9 = (bf16[256,1024]{1,0:T(8,128)(2,1)S(1)}, bf16[256,1024]{1,0:T(8,128)(2,1)S(1)}, u32[]{:S(2)}, u32[]{:S(2)}) collective-permute-start(bf16[256,1024]{1,0:T(8,128)(2,1)S(1)} %collective-permute-done.8.refs_1_.refs_23_), channel_id=1, source_target_pairs={{0,1},{1,0},{2,3},{3,2},{4,5},{5,4},{6,7},{7,6},{8,9},{9,8},{10,11... | collective-permute-start | bytes 1572872 | tf_op jit(solution)/shard_map/ppermute | solution.py:686
  63.3 14.3 %collective-permute-start.19 = (bf16[256,1024]{1,0:T(8,128)(2,1)S(1)}, bf16[256,1024]{1,0:T(8,128)(2,1)S(1)}, u32[]{:S(2)}, u32[]{:S(2)}) collective-permute-start(bf16[256,1024]{1,0:T(8,128)(2,1)S(1)} %up_join.1), channel_id=1, source_target_pairs={{0,2},{1,3},{2,0},{3,1},{4,6},{5,7},{6,4},{7,5},{8,10},{9,11},{10,... | collective-permute-start | bytes 1572872 | tf_op jit(solution)/shard_map/ppermute | solution.py:689
  80.6 8.1 %collective-permute-start.20 = (bf16[256,256]{1,0:T(8,128)(2,1)S(1)}, bf16[256,256]{1,0:T(8,128)(2,1)S(1)}, u32[]{:S(2)}, u32[]{:S(2)}) collective-permute-start(bf16[256,256]{1,0:T(8,128)(2,1)S(1)} %get-tuple-element.219), channel_id=1, source_target_pairs={{0,1},{1,0},{2,3},{3,2},{4,5},{5,4},{6,7},{7,6},{8,9},{9,8},{10,11... | collective-permute-start | bytes 393224 | tf_op jit(solution)/shard_map/ppermute | solution.py:686
  86.0 10.1 %collective-permute-start.29 = (bf16[32,2176]{1,0:T(8,128)(2,1)S(1)}, bf16[32,2176]{1,0:T(8,128)(2,1)S(1)}, u32[]{:S(2)}, u32[]{:S(2)}) collective-permute-start(bf16[32,2176]{1,0:T(8,128)(2,1)S(1)} %get-tuple-element.246), channel_id=1, source_target_pairs={{0,16},{4,20},{8,24},{12,28},{16,0},{20,4},{24,8},{28,12},{1,17},{... | collective-permute-start | bytes 417800 | tf_op jit(solution)/shard_map/ppermute | solution.py:723
  96.1 12.5 %collective-permute-start.32 = (bf16[64,2176]{1,0:T(8,128)(2,1)S(1)}, bf16[64,2176]{1,0:T(8,128)(2,1)S(1)}, u32[]{:S(2)}, u32[]{:S(2)}) collective-permute-start(bf16[64,2176]{1,0:T(8,128)(2,1)S(1)} %get-tuple-element.299), channel_id=1, source_target_pairs={{0,4},{4,0},{8,12},{12,8},{16,20},{20,16},{24,28},{28,24},{1,5},{5... | collective-permute-start | bytes 835592 | tf_op jit(solution)/shard_map/ppermute | solution.py:723
  97.1 11.5 %collective-permute-start.31 = (bf16[64,2176]{1,0:T(8,128)(2,1)S(1)}, bf16[64,2176]{1,0:T(8,128)(2,1)S(1)}, u32[]{:S(2)}, u32[]{:S(2)}) collective-permute-start(bf16[64,2176]{1,0:T(8,128)(2,1)S(1)} %get-tuple-element.299), channel_id=1, source_target_pairs={{0,8},{4,12},{8,0},{12,4},{16,24},{20,28},{24,16},{28,20},{1,9},{5... | collective-permute-start | bytes 835592 | tf_op jit(solution)/shard_map/ppermute | solution.py:723
  98.8 9.8 %collective-permute-start.28 = (bf16[128,1024]{1,0:T(8,128)(2,1)S(1)}, bf16[128,1024]{1,0:T(8,128)(2,1)S(1)}, u32[]{:S(2)}, u32[]{:S(2)}) collective-permute-start(bf16[128,1024]{1,0:T(8,128)(2,1)S(1)} %slice.32), channel_id=1, source_target_pairs={{0,2},{1,3},{2,0},{3,1},{4,6},{5,7},{6,4},{7,5},{8,10},{9,11},{10,... | collective-permute-start | bytes 786440 | tf_op jit(solution)/shard_map/ppermute | solution.py:689
  100.2 8.3 %collective-permute-start.30 = (bf16[32,1152]{1,0:T(8,128)(2,1)S(1)}, bf16[32,1152]{1,0:T(8,128)(2,1)S(1)}, u32[]{:S(2)}, u32[]{:S(2)}) collective-permute-start(bf16[32,1152]{1,0:T(8,128)(2,1)S(1)} %pack_wide.1), channel_id=1, source_target_pairs={{0,16},{4,20},{8,24},{12,28},{16,0},{20,4},{24,8},{28,12},{1,17},{... | collective-permute-start | bytes 221192 | tf_op jit(solution)/shard_map/ppermute | solution.py:723
  113.3 9.1 %collective-permute-start.39 = (bf16[64,2176]{1,0:T(8,128)(2,1)S(1)}, bf16[64,2176]{1,0:T(8,128)(2,1)S(1)}, u32[]{:S(2)}, u32[]{:S(2)}) collective-permute-start(bf16[64,2176]{1,0:T(8,128)(2,1)S(1)} %collective-permute-done.31), channel_id=1, source_target_pairs={{0,4},{4,0},{8,12},{12,8},{16,20},{20,16},{24,28},{28,24},{1,5},{5... | collective-permute-start | bytes 835592 | tf_op jit(solution)/shard_map/ppermute | solution.py:723
  116.9 9.0 %collective-permute-start.38 = (bf16[128,1024]{1,0:T(8,128)(2,1)S(1)}, bf16[128,1024]{1,0:T(8,128)(2,1)S(1)}, u32[]{:S(2)}, u32[]{:S(2)}) collective-permute-start(bf16[128,1024]{1,0:T(8,128)(2,1)S(1)} %slice.33), channel_id=1, source_target_pairs={{0,2},{1,3},{2,0},{3,1},{4,6},{5,7},{6,4},{7,5},{8,10},{9,11},{10,... | collective-permute-start | bytes 786440 | tf_op jit(solution)/shard_map/ppermute | solution.py:689
  117.7 8.2 %collective-permute-start.42 = (bf16[32,1152]{1,0:T(8,128)(2,1)S(1)}, bf16[32,1152]{1,0:T(8,128)(2,1)S(1)}, u32[]{:S(2)}, u32[]{:S(2)}) collective-permute-start(bf16[32,1152]{1,0:T(8,128)(2,1)S(1)} %pack_late.1), channel_id=1, source_target_pairs={{0,16},{4,20},{8,24},{12,28},{16,0},{20,4},{24,8},{28,12},{1,17},{... | collective-permute-start | bytes 221192 | tf_op jit(solution)/shard_map/ppermute | solution.py:723
  119.3 29.2 %collective-permute-start.23 = (bf16[256,1024]{1,0:T(8,128)(2,1)S(1)}, bf16[256,1024]{1,0:T(8,128)(2,1)S(1)}, u32[]{:S(2)}, u32[]{:S(2)}) collective-permute-start(bf16[256,1024]{1,0:T(8,128)(2,1)S(1)} %slice.26), channel_id=1, source_target_pairs={{0,1},{1,0},{2,3},{3,2},{4,5},{5,4},{6,7},{7,6},{8,9},{9,8},{10,11... | collective-permute-start | bytes 1572872 | tf_op jit(solution)/shard_map/ppermute | solution.py:686
  127.9 8.6 %collective-permute-start.49 = (bf16[128,1152]{1,0:T(8,128)(2,1)S(1)}, bf16[128,1152]{1,0:T(8,128)(2,1)S(1)}, u32[]{:S(2)}, u32[]{:S(2)}) collective-permute-start(bf16[128,1152]{1,0:T(8,128)(2,1)S(1)} %pad_maximum_fusion.3), channel_id=1, source_target_pairs={{0,4},{4,0},{8,12},{12,8},{16,20},{20,16},{24,28},{28,24},{1,5},{5... | collective-permute-start | bytes 884744 | tf_op jit(solution)/shard_map/ppermute | solution.py:723
  129.2 10.5 %collective-permute-start.45 = (bf16[256,1024]{1,0:T(8,128)(2,1)S(1)}, bf16[256,1024]{1,0:T(8,128)(2,1)S(1)}, u32[]{:S(2)}, u32[]{:S(2)}) collective-permute-start(bf16[256,1024]{1,0:T(8,128)(2,1)S(1)} %slice.34), channel_id=1, source_target_pairs={{0,1},{1,0},{2,3},{3,2},{4,5},{5,4},{6,7},{7,6},{8,9},{9,8},{10,11... | collective-permute-start | bytes 1572872 | tf_op jit(solution)/shard_map/ppermute | solution.py:686
  134.0 8.4 %collective-permute-start.44 = (bf16[128,1152]{1,0:T(8,128)(2,1)S(1)}, bf16[128,1152]{1,0:T(8,128)(2,1)S(1)}, u32[]{:S(2)}, u32[]{:S(2)}) collective-permute-start(bf16[128,1152]{1,0:T(8,128)(2,1)S(1)} %pad_maximum_fusion.2), channel_id=1, source_target_pairs={{0,4},{4,0},{8,12},{12,8},{16,20},{20,16},{24,28},{28,24},{1,5},{5... | collective-permute-start | bytes 884744 | tf_op jit(solution)/shard_map/ppermute | solution.py:723
  139.0 9.5 %collective-permute-start.41 = (bf16[128,1024]{1,0:T(8,128)(2,1)S(1)}, bf16[128,1024]{1,0:T(8,128)(2,1)S(1)}, u32[]{:S(2)}, u32[]{:S(2)}) collective-permute-start(bf16[128,1024]{1,0:T(8,128)(2,1)S(1)} %slice.30), channel_id=1, source_target_pairs={{0,2},{1,3},{2,0},{3,1},{4,6},{5,7},{6,4},{7,5},{8,10},{9,11},{10,... | collective-permute-start | bytes 786440 | tf_op jit(solution)/shard_map/ppermute | solution.py:689
  (46 other events, 269.5 us)
where the time goes:
time: 154 us
  Pallas kernels  79 us (51%)
  starting transfers between devices  40.7 us (26%)
  waiting for transfers between devices  29.1 us (19%)
  local copies, waits for them, and re-layouts  3.28 us (2%)
    pallas_call x30, Pallas kernels, whole_call(): pl.pallas_call(body, out_shape=kinds, in_specs=[smem_spec] * len(smem) +...  79 us
    ppermute x11, starting transfers between devices, dp_swap(): return lax.ppermute(value, 'dp', [(i, i ^ stride) for i in range(dp_size)])  16.1 us
    ppermute x11, waiting for transfers between devices, dp_swap(): return lax.ppermute(value, 'dp', [(i, i ^ stride) for i in range(dp_size)])  15.1 us
    ppermute x12, starting transfers between devices, chip_hop(): lax.ppermute(value, 'tensor', [(t, (t // 2 + k) % chips * 2 + t % 2) for...  14.8 us
    ppermute x12, waiting for transfers between devices, chip_hop(): lax.ppermute(value, 'tensor', [(t, (t // 2 + k) % chips * 2 + t % 2) for...  12.7 us
    ppermute x24, starting transfers between devices, core_swap(): return lax.ppermute(value, 'tensor', core_perm)  4.84 us
  transfers between devices with their start and end apart: 53, of which 17 were waited for; matrix products, arithmetic and copies ran while one was open for 0% of the time, Pallas kernels for 44%

commit v1 on v0

--- a/solution.py
+++ b/solution.py
@@ -386,13 +386,14 @@
         grad_mid[part, :] = total
         attn = total.astype(BF)
         grad_attn[part, :] = attn
-        low = (dot_back(attn, proj_out[...]) * mask[part, :]).astype(BF)
-        grad_low[part, :] = low
-        value = (dot_back(attn, w_all[...]) + dot(low, in_all[...])).astype(BF)
-        for d in range(count[1]):
-            outs[d][part, :] = value[:, d * width : (d + 1) * width]
 
     repeat(2, one)
+    attn = grad_attn[...]
+    low = (dot_back(attn, proj_out[...]) * mask[pl.ds(0, 2 * half), :]).astype(BF)
+    grad_low[...] = low
+    value = (dot_back(attn, w_all[...]) + dot(low, in_all[...])).astype(BF)
+    for d in range(count[1]):
+        outs[d][...] = value[:, d * width : (d + 1) * width]
 
 
 def message_body(count, pairs, me, up_in, down_out, proj_low, grad_attn, grad_low, *refs):
@@ -1001,14 +1002,6 @@
         scratch=[pltpu.VMEM((own, wide), F32)],
         final=(0,),
     )
-    up_in_full, down_out_full, proj_out_full = whole_call(
-        functools.partial(place_wide_body, count),
-        [tie(wide_blocks[0], grad_input)] + wide_blocks[1:],
-        [shape((wide, cols), F32), shape((cols, wide), F32), shape((cols, wide), F32)],
-        "place_wide",
-        smem=[place],
-        final=(0, 1, 2),
-    )
     late_found = widen(double(late_found, tie(late_moved, grad_input)), top // 8)
     qkv_out_full, late_part = whole_call(
         functools.partial(spread_late_body, width),
@@ -1017,15 +1010,9 @@
         "spread_late",
         final=(0,),
     )
-    late_blocks = weave(late_part, core_swap(late_part), hops_of(late_part))
-    (result,) = whole_call(
-        result_body,
-        [mid, row(down_bias), down_mine, down_swap, *down_first, *[tie(item, late_part) for item in down_second]],
-        [shape((own, wide), F32)],
-        "result",
-        final=(0,),
-    )
-    hidden_found = jnp.concatenate([hidden_half, hidden_moved, hidden_first, tie(hidden_second, result)], 0)
+    late_swap = core_swap(late_part)
+    late_hops = hops_of(late_part)
+    hidden_found = jnp.concatenate([hidden_half, hidden_moved, hidden_first, tie(hidden_second, late_part)], 0)
     up_out_full, down_in_full = whole_call(
         functools.partial(spread_hidden_body, hid),
         [widen(hidden_found, top // 8)],
@@ -1033,9 +1020,25 @@
         "spread_hidden",
         final=(0, 1),
     )
+    up_in_full, down_out_full, proj_out_full = whole_call(
+        functools.partial(place_wide_body, count),
+        [tie(wide_blocks[0], up_out_full)] + wide_blocks[1:],
+        [shape((wide, cols), F32), shape((cols, wide), F32), shape((cols, wide), F32)],
+        "place_wide",
+        smem=[place],
+        final=(0, 1, 2),
+    )
+    late_blocks = weave(late_part, late_swap, [tie(item, up_in_full) for item in late_hops])
+    (result,) = whole_call(
+        result_body,
+        [mid, row(down_bias), down_mine, down_swap, *down_first, *[tie(item, up_in_full) for item in down_second]],
+        [shape((own, wide), F32)],
+        "result",
+        final=(0,),
+    )
     (qkv_in_full,) = whole_call(
         functools.partial(place_late_body, count),
-        [late_blocks[0]] + [tie(item, up_out_full) for item in late_blocks[1:]],
+        late_blocks,
         [shape((wide, cols), F32)],
         "place_late",
         smem=[place],

time: 154 us -> 151 us (0.981)
  transfers between devices with their start and end apart: 53 -> 53, of which waited for: 17 -> 16; matrix products, arithmetic and copies ran while one was open for 0% -> 0% of each run, Pallas kernels for 44% -> 45%
where the time goes in v1:
time: 151 us
  Pallas kernels  78.3 us (52%)
  starting transfers between devices  39.4 us (26%)
  waiting for transfers between devices  28 us (19%)
  local copies, waits for them, and re-layouts  3.28 us (2%)
    pallas_call x30, Pallas kernels, whole_call(): pl.pallas_call(body, out_shape=kinds, in_specs=[smem_spec] * len(smem) +...  78.3 us
    ppermute x11, starting transfers between devices, dp_swap(): return lax.ppermute(value, 'dp', [(i, i ^ stride) for i in range(dp_size)])  16.5 us
    ppermute x11, waiting for transfers between devices, dp_swap(): return lax.ppermute(value, 'dp', [(i, i ^ stride) for i in range(dp_size)])  14 us
    ppermute x12, starting transfers between devices, chip_hop(): lax.ppermute(value, 'tensor', [(t, (t // 2 + k) % chips * 2 + t % 2) for...  13.4 us
    ppermute x12, waiting for transfers between devices, chip_hop(): lax.ppermute(value, 'tensor', [(t, (t // 2 + k) % chips * 2 + t % 2) for...  12.7 us
    ppermute x24, starting transfers between devices, core_swap(): return lax.ppermute(value, 'tensor', core_perm)  4.38 us
    unnamed x38, local copies, waits for them, and re-layouts  3.06 us
  transfers between devices with their start and end apart: 53, of which 16 were waited for; matrix products, arithmetic and copies ran while one was open for 0% of the time, Pallas kernels for 45%

profile of v1, /device:TPU:0, one launch (start us, length us, event | category | flops | bytes accessed | tf_op | source)
XLA Modules:
  0.0 150.6 jit_solution(9347810178561895455)
XLA Ops:
  1.2 2.6 %collective-permute-start.1 = (bf16[256,1024]{1,0:T(8,128)(2,1)}, bf16[256,1024]{1,0:T(8,128)(2,1)S(1)}, u32[]{:S(2)}, u32[]{:S(2)}) collective-permute-start(bf16[256,1024]{1,0:T(8,128)(2,1)} %tokens.1), channel_id=1, source_target_pairs={{0,2},{1,3},{2,0},{3,1},{4,6},{5,7},{6,4},{7,5},{8,10},{9,11},{10,... | collective-permute-start | bytes 1572872 | tf_op jit(solution)/shard_map/ppermute | solution.py:690
  5.0 3.9 %prep.1 = (bf16[32,1024]{1,0:T(8,128)(2,1)S(1)}, bf16[3,32,256]{2,1,0:T(8,128)(2,1)S(1)}, bf16[272,1024]{1,0:T(8,128)(2,1)S(1)}, bf16[32,1024]{1,0:T(8,128)(2,1)...) custom-call(s32[1]{0:T(128)} %bitcast.me.refs_0_, ...), custom_call_target="tpu_custom_call" | custom-call | tf_op jit(solution)/shard_map/prep/pallas_call | solution.py:46
  9.8 6.2 %qkv_near.1 = (bf16[512,1024]{1,0:T(8,128)(2,1)S(1)}, bf16[512,32]{1,0:T(8,128)(2,1)S(1)}, f32[1024,768]{1,0:T(8,128)S(1)}) custom-call(f32[1024,32]{1,0:T(8,128)S(1)} %get-tuple-element.184.mask, f32[1,1024]{1,0:T(1,128)} %bitcast.28, f32[1,1024]{1,0:T(1,128)} %bitcast.31, bf16[3,1024,256]{2,1,0:T(8,128)(2,1)} %bitcast.12, f32[2,256]{1,0:T(2,128)} %bias.3, ...), custom_call_target="tpu_custom_call" | custom-call | tf_op jit(solution)/shard_map/qkv_near/pallas_call | solution.py:46
  16.5 1.8 %collective-permute-start.4 = (bf16[144,1024]{1,0:T(8,128)(2,1)S(1)}, bf16[144,1024]{1,0:T(8,128)(2,1)S(1)}, u32[]{:S(2)}, u32[]{:S(2)}) collective-permute-start(bf16[144,1024]{1,0:T(8,128)(2,1)S(1)} %get-tuple-element.163), channel_id=1, source_target_pairs={{0,2},{1,3},{2,0},{3,1},{4,6},{5,7},{6,4},{7,5},{8,10},{9,11},{10,... | collective-permute-start | bytes 884744 | tf_op jit(solution)/shard_map/ppermute | solution.py:690
  18.6 4.4 %qkv_far.1 = (bf16[512,1024]{1,0:T(8,128)(2,1)S(1)}, bf16[512,32]{1,0:T(8,128)(2,1)S(1)}, bf16[1024,768]{1,0:T(8,128)(2,1)S(1)}) custom-call(f32[1024,32]{1,0:T(8,128)S(1)} %get-tuple-element.184.mask, f32[1,1024]{1,0:T(1,128)S(1)} %bitcast.29, f32[1,1024]{1,0:T(1,128)S(1)} %bitcast.32, bf16[3,1024,256]{2,1,0:T(8,128)(2,1)S(1)} %bitcast.13, ...), custom_call_target="tpu_custom_call" | custom-call | tf_op jit(solution)/shard_map/qkv_far/pallas_call | solution.py:46
  24.6 4.4 %attend0.1 = (bf16[1024,128]{1,0:T(8,128)(2,1)S(1)}, bf16[2,2,512,512]{3,2,1,0:T(8,128)(2,1)S(1)}) custom-call(s32[1,1024]{1,0:T(1,128)S(1)} %get-tuple-element.164.limit, bf16[1024,768]{1,0:T(8,128)(2,1)S(1)} %get-tuple-element.167.seq.refs_0_.refs_1_, bf16[1024,1024]{1,0:T(8,128)(2,1)S(1)} %get-tuple-element.161.push.refs_4_), custom_call_target="tpu_custom_call" | custom-call | tf_op jit(solution)/shard_map/attend0/pallas_call | solution.py:46
  29.0 4.4 %attend1.1 = (bf16[1024,128]{1,0:T(8,128)(2,1)S(1)}, bf16[2,2,512,512]{3,2,1,0:T(8,128)(2,1)S(1)}) custom-call(s32[1,1024]{1,0:T(1,128)S(1)} %get-tuple-element.164.limit, bf16[1024,768]{1,0:T(8,128)(2,1)S(1)} %get-tuple-element.167.seq.refs_0_.refs_1_, bf16[1024,1024]{1,0:T(8,128)(2,1)S(1)} %get-tuple-element.161.push.refs_4_), custom_call_target="tpu_custom_call" | custom-call | tf_op jit(solution)/shard_map/attend1/pallas_call | solution.py:46
  35.6 6.0 %collective-permute-done.5.refs_3_ = bf16[128,1024]{1,0:T(8,128)(2,1)S(1)} collective-permute-done((bf16[128,1024]{1,0:T(8,128)(2,1)S(1)}, bf16[128,1024]{1,0:T(8,128)(2,1)S(1)}, u32[]{:S(2)}, u32[]{:S(2)}) %collective-permute-start.5) | collective-permute-done | bytes 262176 | tf_op jit(solution)/shard_map/ppermute | solution.py:724
  44.2 5.2 %collective-permute-done.13.refs_7_.refs_9_.refs_5_ = bf16[1024,128]{1,0:T(8,128)(2,1)S(1)} collective-permute-done((bf16[1024,128]{1,0:T(8,128)(2,1)S(1)}, bf16[1024,128]{1,0:T(8,128)(2,1)S(1)}, u32[]{:S(2)}, u32[]{:S(2)}) %collective-permute-start.13) | collective-permute-done | bytes 262176 | tf_op jit(solution)/shard_map/ppermute | solution.py:690
  52.2 5.2 %block_odd.1 = (bf16[256,1024]{1,0:T(8,128)(2,1)S(1)}, bf16[256,1024]{1,0:T(8,128)(2,1)S(1)}, bf16[256,32]{1,0:T(8,128)(2,1)S(1)}, bf16[256,32]{1,0:T(8,128)(2,1...) custom-call(f32[1024,32]{1,0:T(8,128)S(1)} %get-tuple-element.184.ma, ...), custom_call_target="tpu_custom_call" | custom-call | tf_op jit(solution)/shard_map/block_odd/pallas_call | solution.py:46
  58.1 5.1 %block_even.1 = (bf16[256,1024]{1,0:T(8,128)(2,1)S(1)}, bf16[256,1024]{1,0:T(8,128)(2,1)S(1)}, bf16[256,32]{1,0:T(8,128)(2,1)S(1)}, bf16[256,32]{1,0:T(8,128)(2,...) custom-call(f32[1024,32]{1,0:T(8,128)S(1)} %get-tuple-element.184.ma, ...), custom_call_target="tpu_custom_call" | custom-call | tf_op jit(solution)/shard_map/block_even/pallas_call | solution.py:46
  64.3 10.5 %block_near.1 = (bf16[512,1024]{1,0:T(8,128)(2,1)S(1)}, bf16[512,1024]{1,0:T(8,128)(2,1)S(1)}, bf16[512,32]{1,0:T(8,128)(2,1)S(1)}, bf16[512,32]{1,0:T(8,128)(2,...) custom-call(f32[1024,32]{1,0:T(8,128)S(1)} %get-tuple-element.184.ma, ...), custom_call_target="tpu_custom_call" | custom-call | tf_op jit(solution)/shard_map/block_near/pallas_call | solution.py:46
  77.6 2.2 %mid_back.1 = (f32[256,1024]{1,0:T(8,128)S(1)}, bf16[256,1024]{1,0:T(8,128)(2,1)S(1)}, bf16[256,32]{1,0:T(8,128)(2,1)S(1)}, bf16[256,256]{1,0:T(8,128)(2,1)S(1)}...) custom-call(f32[1024,32]{1,0:T(8,128)S(1)} %get-tuple-element.184.mask, ...), custom_call_target="tpu_custom_call" | custom-call | tf_op jit(solution)/shard_map/mid_back/pallas_call | solution.py:46
  82.2 3.1 %down.1 = (bf16[512,1024]{1,0:T(8,128)(2,1)S(1)}, bf16[256,1024]{1,0:T(8,128)(2,1)S(1)}, bf16[256,1024]{1,0:T(8,128)(2,1)S(1)}) custom-call(bf16[1024,1024]{1,0:T(8,128)(2,1)S(1)} %copy-done, bf16[32,1024]{1,0:T(8,128)(2,1)S(1)} %get-tuple-element.176.down_out, bf16[512,1024]{1,0:T(8,128)(2,1)S(1)} %get-tuple-element.196.refs_9_.refs_0_, ...), custom_call_target="tpu_custom_call" | custom-call | tf_op jit(solution)/shard_map/down/pallas_call | solution.py:46
  85.3 2.7 %collective-permute-start.29 = (bf16[32,2176]{1,0:T(8,128)(2,1)S(1)}, bf16[32,2176]{1,0:T(8,128)(2,1)S(1)}, u32[]{:S(2)}, u32[]{:S(2)}) collective-permute-start(bf16[32,2176]{1,0:T(8,128)(2,1)S(1)} %get-tuple-element.244), channel_id=1, source_target_pairs={{0,16},{4,20},{8,24},{12,28},{16,0},{20,4},{24,8},{28,12},{1,17},{... | collective-permute-start | bytes 417800 | tf_op jit(solution)/shard_map/ppermute | solution.py:724
  90.6 4.7 %attend_back0.1 = (bf16[128,1024]{1,0:T(8,128)(2,1)S(1)}, bf16[1024,128]{1,0:T(8,128)(2,1)S(1)}, bf16[1024,128]{1,0:T(8,128)(2,1)S(1)}, bf16[1024,256]{1,0:T(8,128)(2,1)S(1)}) custom-call(bf16[1024,768]{1,0:T(8,128)(2,1)S(1)} %get-tuple-element.167.seq.refs_0_.refs_1_, bf16[2,2,512,512]{3,2,1,0:T(8,128)(2,1)S(1)} %get-tuple-element.227.refs_1_, ...), custom_call_target="tpu_custom_call" | custom-call | tf_op jit(solution)/shard_map/attend_back0/pallas_call | solution.py:46
  99.5 2.7 %collective-permute-start.30 = (bf16[32,1152]{1,0:T(8,128)(2,1)S(1)}, bf16[32,1152]{1,0:T(8,128)(2,1)S(1)}, u32[]{:S(2)}, u32[]{:S(2)}) collective-permute-start(bf16[32,1152]{1,0:T(8,128)(2,1)S(1)} %pack_wide.1), channel_id=1, source_target_pairs={{0,16},{4,20},{8,24},{12,28},{16,0},{20,4},{24,8},{28,12},{1,17},{... | collective-permute-start | bytes 221192 | tf_op jit(solution)/shard_map/ppermute | solution.py:724
  102.2 5.7 %attend_back1.1 = (bf16[256,1024]{1,0:T(8,128)(2,1)S(1)}, bf16[1024,256]{1,0:T(8,128)(2,1)S(1)}, bf16[1024,256]{1,0:T(8,128)(2,1)S(1)}, bf16[32,1024]{1,0:T(8,12...) custom-call(s32[1]{0:T(128)} %bitcast.me.refs_0_, ...), custom_call_target="tpu_custom_call" | custom-call | tf_op jit(solution)/shard_map/attend_back1/pallas_call | solution.py:46
  119.8 2.0 %collective-permute-done.39 = bf16[64,2176]{1,0:T(8,128)(2,1)S(1)} collective-permute-done((bf16[64,2176]{1,0:T(8,128)(2,1)S(1)}, bf16[64,2176]{1,0:T(8,128)(2,1)S(1)}, u32[]{:S(2)}, u32[]{:S(2)}) %collective-permute-start.39) | collective-permute-done | bytes 278560 | tf_op jit(solution)/shard_map/ppermute | solution.py:724
  121.8 3.5 %qkv_back_near.1.refs_0_ = bf16[512,1024]{1,0:T(8,128)(2,1)S(1)} custom-call(bf16[1024,1024]{1,0:T(8,128)(2,1)S(1)} %get-tuple-element.161.push.refs_4_, bf16[1024,768]{1,0:T(8,128)(2,1)S(1)} %get-tuple-element.254.w_cat, bf16[32,1024]{1,0:T(8,128)(2,1)S(1)} %get-tuple-element.153.low_in, bf16[256,1024]{1,0:T(8,128)(2,1)S(1)} %get-tuple-element.255.grad_q, ...), custom_call_target="tpu_custom_call" | custom-call | tf_op jit(solution)/shard_map/qkv_back_near/pallas_call | solution.py:46
  127.3 3.5 %collective-permute-done.44 = bf16[64,1152]{1,0:T(8,128)(2,1)S(1)} collective-permute-done((bf16[64,1152]{1,0:T(8,128)(2,1)S(1)}, bf16[64,1152]{1,0:T(8,128)(2,1)S(1)}, u32[]{:S(2)}, u32[]{:S(2)}) %collective-permute-start.44) | collective-permute-done | bytes 147488 | tf_op jit(solution)/shard_map/ppermute | solution.py:724
  130.8 3.3 %collective-permute-done.40.refs_3_ = bf16[128,1024]{1,0:T(8,128)(2,1)S(1)} collective-permute-done((bf16[128,1024]{1,0:T(8,128)(2,1)S(1)}, bf16[128,1024]{1,0:T(8,128)(2,1)S(1)}, u32[]{:S(2)}, u32[]{:S(2)}) %collective-permute-start.40) | collective-permute-done | bytes 262176 | tf_op jit(solution)/shard_map/ppermute | solution.py:690
  137.9 1.9 %input_back.1 = f32[256,1024]{1,0:T(8,128)} custom-call(bf16[256,1024]{1,0:T(8,128)(2,1)S(1)} %copy-done.3, f32[256,1024]{1,0:T(8,128)S(1)} %get-tuple-element.280.grad_mid, f32[1,1024]{1,0:T(1,128)S(1)} %bitcast.30, bf16[512,1024]{1,0:T(8,128)(2,1)S(1)} %qkv_back_near.1.refs_0_, bf16[256,1024]{1,0:T(8,128)(2,1)S(1)} %collective-permute-done.46.refs_1_, ...), custom_call_target="tpu_custom_call" | custom-call | tf_op jit(solution)/shard_map/input_back/pallas_call | solution.py:46
  141.0 1.9 %collective-permute-done.45 = bf16[128,1152]{1,0:T(8,128)(2,1)S(1)} collective-permute-done((bf16[128,1152]{1,0:T(8,128)(2,1)S(1)}, bf16[128,1152]{1,0:T(8,128)(2,1)S(1)}, u32[]{:S(2)}, u32[]{:S(2)}) %collective-permute-start.45) | collective-permute-done | bytes 294944 | tf_op jit(solution)/shard_map/ppermute | solution.py:724
  (166 shorter events, 52.6 us)
Async XLA Ops:
  0.6 8.3 %collective-permute-start = (bf16[256,1024]{1,0:T(8,128)(2,1)}, bf16[256,1024]{1,0:T(8,128)(2,1)S(1)}, u32[]{:S(2)}, u32[]{:S(2)}) collective-permute-start(bf16[256,1024]{1,0:T(8,128)(2,1)} %tokens.1), channel_id=1, source_target_pairs={{0,1},{1,0},{2,3},{3,2},{4,5},{5,4},{6,7},{7,6},{8,9},{9,8},{10,11... | collective-permute-start | bytes 1572872 | tf_op jit(solution)/shard_map/ppermute | solution.py:687
  1.2 15.3 %collective-permute-start.1 = (bf16[256,1024]{1,0:T(8,128)(2,1)}, bf16[256,1024]{1,0:T(8,128)(2,1)S(1)}, u32[]{:S(2)}, u32[]{:S(2)}) collective-permute-start(bf16[256,1024]{1,0:T(8,128)(2,1)} %tokens.1), channel_id=1, source_target_pairs={{0,2},{1,3},{2,0},{3,1},{4,6},{5,7},{6,4},{7,5},{8,10},{9,11},{10,... | collective-permute-start | bytes 1572872 | tf_op jit(solution)/shard_map/ppermute | solution.py:690
  16.5 17.0 %collective-permute-start.4 = (bf16[144,1024]{1,0:T(8,128)(2,1)S(1)}, bf16[144,1024]{1,0:T(8,128)(2,1)S(1)}, u32[]{:S(2)}, u32[]{:S(2)}) collective-permute-start(bf16[144,1024]{1,0:T(8,128)(2,1)S(1)} %get-tuple-element.163), channel_id=1, source_target_pairs={{0,2},{1,3},{2,0},{3,1},{4,6},{5,7},{6,4},{7,5},{8,10},{9,11},{10,... | collective-permute-start | bytes 884744 | tf_op jit(solution)/shard_map/ppermute | solution.py:690
  18.2 24.0 %collective-permute-start.3 = (bf16[272,1024]{1,0:T(8,128)(2,1)S(1)}, bf16[272,1024]{1,0:T(8,128)(2,1)S(1)}, u32[]{:S(2)}, u32[]{:S(2)}) collective-permute-start(bf16[272,1024]{1,0:T(8,128)(2,1)S(1)} %get-tuple-element.162.refs_0_), channel_id=1, source_target_pairs={{0,1},{1,0},{2,3},{3,2},{4,5},{5,4},{6,7},{7,6},{8,9},{9,8},{10,11... | collective-permute-start | bytes 1671176 | tf_op jit(solution)/shard_map/ppermute | solution.py:687
  23.0 19.3 %collective-permute-start.8 = (bf16[256,1024]{1,0:T(8,128)(2,1)S(1)}, bf16[256,1024]{1,0:T(8,128)(2,1)S(1)}, u32[]{:S(2)}, u32[]{:S(2)}) collective-permute-start(bf16[256,1024]{1,0:T(8,128)(2,1)S(1)} %convert_element_type.3.refs_2_.refs_21_), channel_id=1, source_target_pairs={{0,2},{1,3},{2,0},{3,1},{4,6},{5,7},{6,4},{7,5},{8,10},{9,11},{10,... | collective-permute-start | bytes 1572872 | tf_op jit(solution)/shard_map/ppermute | solution.py:690
  33.5 8.1 %collective-permute-start.5 = (bf16[128,1024]{1,0:T(8,128)(2,1)S(1)}, bf16[128,1024]{1,0:T(8,128)(2,1)S(1)}, u32[]{:S(2)}, u32[]{:S(2)}) collective-permute-start(bf16[128,1024]{1,0:T(8,128)(2,1)S(1)} %slice.24), channel_id=1, source_target_pairs={{0,4},{4,0},{8,12},{12,8},{16,20},{20,16},{24,28},{28,24},{1,5},{5... | collective-permute-start | bytes 786440 | tf_op jit(solution)/shard_map/ppermute | solution.py:724
  35.1 14.3 %collective-permute-start.6 = (bf16[144,1024]{1,0:T(8,128)(2,1)S(1)}, bf16[144,1024]{1,0:T(8,128)(2,1)S(1)}, u32[]{:S(2)}, u32[]{:S(2)}) collective-permute-start(bf16[144,1024]{1,0:T(8,128)(2,1)S(1)} %collective-permute-done.4.refs_2_), channel_id=1, source_target_pairs={{0,1},{1,0},{2,3},{3,2},{4,5},{5,4},{6,7},{7,6},{8,9},{9,8},{10,11... | collective-permute-start | bytes 884744 | tf_op jit(solution)/shard_map/ppermute | solution.py:687
  35.1 9.1 %collective-permute-start.12 = (bf16[1024,128]{1,0:T(8,128)(2,1)S(1)}, bf16[1024,128]{1,0:T(8,128)(2,1)S(1)}, u32[]{:S(2)}, u32[]{:S(2)}) collective-permute-start(bf16[1024,128]{1,0:T(8,128)(2,1)S(1)} %get-tuple-element.166.refs_2_.refs_4_.refs_0_), channel_id=1, source_target_pairs={{0,2},{1,3},{2,0},{3,1},{4,6},{5,7},{6,4},{7,5},{8,10},{9,11},{10,... | collective-permute-start | bytes 786440 | tf_op jit(solution)/shard_map/ppermute | solution.py:690
  42.3 9.5 %collective-permute-start.9 = (bf16[256,1024]{1,0:T(8,128)(2,1)S(1)}, bf16[256,1024]{1,0:T(8,128)(2,1)S(1)}, u32[]{:S(2)}, u32[]{:S(2)}) collective-permute-start(bf16[256,1024]{1,0:T(8,128)(2,1)S(1)} %collective-permute-done.8.refs_1_.refs_23_), channel_id=1, source_target_pairs={{0,1},{1,0},{2,3},{3,2},{4,5},{5,4},{6,7},{7,6},{8,9},{9,8},{10,11... | collective-permute-start | bytes 1572872 | tf_op jit(solution)/shard_map/ppermute | solution.py:687
  63.3 14.3 %collective-permute-start.19 = (bf16[256,1024]{1,0:T(8,128)(2,1)S(1)}, bf16[256,1024]{1,0:T(8,128)(2,1)S(1)}, u32[]{:S(2)}, u32[]{:S(2)}) collective-permute-start(bf16[256,1024]{1,0:T(8,128)(2,1)S(1)} %up_join.1), channel_id=1, source_target_pairs={{0,2},{1,3},{2,0},{3,1},{4,6},{5,7},{6,4},{7,5},{8,10},{9,11},{10,... | collective-permute-start | bytes 1572872 | tf_op jit(solution)/shard_map/ppermute | solution.py:690
  79.9 8.1 %collective-permute-start.20 = (bf16[256,256]{1,0:T(8,128)(2,1)S(1)}, bf16[256,256]{1,0:T(8,128)(2,1)S(1)}, u32[]{:S(2)}, u32[]{:S(2)}) collective-permute-start(bf16[256,256]{1,0:T(8,128)(2,1)S(1)} %get-tuple-element.217), channel_id=1, source_target_pairs={{0,1},{1,0},{2,3},{3,2},{4,5},{5,4},{6,7},{7,6},{8,9},{9,8},{10,11... | collective-permute-start | bytes 393224 | tf_op jit(solution)/shard_map/ppermute | solution.py:687
  85.3 10.1 %collective-permute-start.29 = (bf16[32,2176]{1,0:T(8,128)(2,1)S(1)}, bf16[32,2176]{1,0:T(8,128)(2,1)S(1)}, u32[]{:S(2)}, u32[]{:S(2)}) collective-permute-start(bf16[32,2176]{1,0:T(8,128)(2,1)S(1)} %get-tuple-element.244), channel_id=1, source_target_pairs={{0,16},{4,20},{8,24},{12,28},{16,0},{20,4},{24,8},{28,12},{1,17},{... | collective-permute-start | bytes 417800 | tf_op jit(solution)/shard_map/ppermute | solution.py:724
  95.4 12.5 %collective-permute-start.32 = (bf16[64,2176]{1,0:T(8,128)(2,1)S(1)}, bf16[64,2176]{1,0:T(8,128)(2,1)S(1)}, u32[]{:S(2)}, u32[]{:S(2)}) collective-permute-start(bf16[64,2176]{1,0:T(8,128)(2,1)S(1)} %get-tuple-element.295), channel_id=1, source_target_pairs={{0,4},{4,0},{8,12},{12,8},{16,20},{20,16},{24,28},{28,24},{1,5},{5... | collective-permute-start | bytes 835592 | tf_op jit(solution)/shard_map/ppermute | solution.py:724
  96.4 11.5 %collective-permute-start.31 = (bf16[64,2176]{1,0:T(8,128)(2,1)S(1)}, bf16[64,2176]{1,0:T(8,128)(2,1)S(1)}, u32[]{:S(2)}, u32[]{:S(2)}) collective-permute-start(bf16[64,2176]{1,0:T(8,128)(2,1)S(1)} %get-tuple-element.295), channel_id=1, source_target_pairs={{0,8},{4,12},{8,0},{12,4},{16,24},{20,28},{24,16},{28,20},{1,9},{5... | collective-permute-start | bytes 835592 | tf_op jit(solution)/shard_map/ppermute | solution.py:724
  98.1 9.8 %collective-permute-start.28 = (bf16[128,1024]{1,0:T(8,128)(2,1)S(1)}, bf16[128,1024]{1,0:T(8,128)(2,1)S(1)}, u32[]{:S(2)}, u32[]{:S(2)}) collective-permute-start(bf16[128,1024]{1,0:T(8,128)(2,1)S(1)} %slice.32), channel_id=1, source_target_pairs={{0,2},{1,3},{2,0},{3,1},{4,6},{5,7},{6,4},{7,5},{8,10},{9,11},{10,... | collective-permute-start | bytes 786440 | tf_op jit(solution)/shard_map/ppermute | solution.py:690
  99.5 8.4 %collective-permute-start.30 = (bf16[32,1152]{1,0:T(8,128)(2,1)S(1)}, bf16[32,1152]{1,0:T(8,128)(2,1)S(1)}, u32[]{:S(2)}, u32[]{:S(2)}) collective-permute-start(bf16[32,1152]{1,0:T(8,128)(2,1)S(1)} %pack_wide.1), channel_id=1, source_target_pairs={{0,16},{4,20},{8,24},{12,28},{16,0},{20,4},{24,8},{28,12},{1,17},{... | collective-permute-start | bytes 221192 | tf_op jit(solution)/shard_map/ppermute | solution.py:724
  112.6 9.2 %collective-permute-start.39 = (bf16[64,2176]{1,0:T(8,128)(2,1)S(1)}, bf16[64,2176]{1,0:T(8,128)(2,1)S(1)}, u32[]{:S(2)}, u32[]{:S(2)}) collective-permute-start(bf16[64,2176]{1,0:T(8,128)(2,1)S(1)} %collective-permute-done.31), channel_id=1, source_target_pairs={{0,4},{4,0},{8,12},{12,8},{16,20},{20,16},{24,28},{28,24},{1,5},{5... | collective-permute-start | bytes 835592 | tf_op jit(solution)/shard_map/ppermute | solution.py:724
  116.2 9.1 %collective-permute-start.38 = (bf16[128,1024]{1,0:T(8,128)(2,1)S(1)}, bf16[128,1024]{1,0:T(8,128)(2,1)S(1)}, u32[]{:S(2)}, u32[]{:S(2)}) collective-permute-start(bf16[128,1024]{1,0:T(8,128)(2,1)S(1)} %slice.33), channel_id=1, source_target_pairs={{0,2},{1,3},{2,0},{3,1},{4,6},{5,7},{6,4},{7,5},{8,10},{9,11},{10,... | collective-permute-start | bytes 786440 | tf_op jit(solution)/shard_map/ppermute | solution.py:690
  117.0 31.3 %collective-permute-start.23 = (bf16[256,1024]{1,0:T(8,128)(2,1)S(1)}, bf16[256,1024]{1,0:T(8,128)(2,1)S(1)}, u32[]{:S(2)}, u32[]{:S(2)}) collective-permute-start(bf16[256,1024]{1,0:T(8,128)(2,1)S(1)} %slice.26), channel_id=1, source_target_pairs={{0,1},{1,0},{2,3},{3,2},{4,5},{5,4},{6,7},{7,6},{8,9},{9,8},{10,11... | collective-permute-start | bytes 1572872 | tf_op jit(solution)/shard_map/ppermute | solution.py:687
  117.1 8.2 %collective-permute-start.43 = (bf16[32,1152]{1,0:T(8,128)(2,1)S(1)}, bf16[32,1152]{1,0:T(8,128)(2,1)S(1)}, u32[]{:S(2)}, u32[]{:S(2)}) collective-permute-start(bf16[32,1152]{1,0:T(8,128)(2,1)S(1)} %pack_late.1), channel_id=1, source_target_pairs={{0,16},{4,20},{8,24},{12,28},{16,0},{20,4},{24,8},{28,12},{1,17},{... | collective-permute-start | bytes 221192 | tf_op jit(solution)/shard_map/ppermute | solution.py:724
  118.6 15.4 %collective-permute-start.42 = (bf16[128,1152]{1,0:T(8,128)(2,1)S(1)}, bf16[128,1152]{1,0:T(8,128)(2,1)S(1)}, u32[]{:S(2)}, u32[]{:S(2)}) collective-permute-start(bf16[128,1152]{1,0:T(8,128)(2,1)S(1)} %pad_maximum_fusion.2), channel_id=1, source_target_pairs={{0,4},{4,0},{8,12},{12,8},{16,20},{20,16},{24,28},{28,24},{1,5},{5... | collective-permute-start | bytes 884744 | tf_op jit(solution)/shard_map/ppermute | solution.py:724
  127.2 10.0 %collective-permute-start.46 = (bf16[256,1024]{1,0:T(8,128)(2,1)S(1)}, bf16[256,1024]{1,0:T(8,128)(2,1)S(1)}, u32[]{:S(2)}, u32[]{:S(2)}) collective-permute-start(bf16[256,1024]{1,0:T(8,128)(2,1)S(1)} %slice.34), channel_id=1, source_target_pairs={{0,1},{1,0},{2,3},{3,2},{4,5},{5,4},{6,7},{7,6},{8,9},{9,8},{10,11... | collective-permute-start | bytes 1572872 | tf_op jit(solution)/shard_map/ppermute | solution.py:687
  137.0 9.6 %collective-permute-start.47 = (bf16[384,256]{1,0:T(8,128)(2,1)S(1)}, bf16[384,256]{1,0:T(8,128)(2,1)S(1)}, u32[]{:S(2)}, u32[]{:S(2)}) collective-permute-start(bf16[384,256]{1,0:T(8,128)(2,1)S(1)} %get-tuple-element.285.refs_0_), channel_id=1, source_target_pairs={{0,1},{1,0},{2,3},{3,2},{4,5},{5,4},{6,7},{7,6},{8,9},{9,8},{10,11... | collective-permute-start | bytes 589832 | tf_op jit(solution)/shard_map/ppermute | solution.py:687
  137.1 11.2 %collective-permute-start.41 = (bf16[128,1024]{1,0:T(8,128)(2,1)S(1)}, bf16[128,1024]{1,0:T(8,128)(2,1)S(1)}, u32[]{:S(2)}, u32[]{:S(2)}) collective-permute-start(bf16[128,1024]{1,0:T(8,128)(2,1)S(1)} %slice.30), channel_id=1, source_target_pairs={{0,2},{1,3},{2,0},{3,1},{4,6},{5,7},{6,4},{7,5},{8,10},{9,11},{10,... | collective-permute-start | bytes 786440 | tf_op jit(solution)/shard_map/ppermute | solution.py:690
  (46 other events, 261.2 us)

commit v2 on v1

--- a/solution.py
+++ b/solution.py
@@ -975,11 +975,11 @@
     late_moved = dp_swap(pack_late, top)
     wide_found = double(wide_found, wide_moved)
     wide_moved = dp_swap(wide_found, top // 4)
-    near_part = unproject(near_ids, [qkv_joined, pack_late, hidden_second], "qkv_back_near")
+    near_part = unproject(near_ids, [qkv_joined, pack_late], "qkv_back_near")
     qkv_swap = core_swap(near_part[own:])
     qkv_first = [tie(item, near_part) for item in qkv_first]
     qkv_second = send_half(tie(qkv_joined, *qkv_first), 1)
-    late_found = double(pack_late, tie(late_moved, near_part, *qkv_first))
+    late_found = double(pack_late, tie(late_moved, near_part, hidden_second, *qkv_first))
     late_moved = dp_swap(late_found, top // 2)
     late_moved = tie(late_moved, *qkv_second)
     wide_found = widen(double(wide_found, tie(wide_moved, late_moved)), top // 8)

time: 151 us -> 149 us (0.987)
  waiting for transfers between devices: 28 us -> 25.7 us
    ppermute x11, waiting for transfers between devices: 14 us -> 12.1 us  [dp_swap(): return lax.ppermute(value, 'dp', [(i, i ^ stride) for i in range(dp_size)])]
  transfers between devices with their start and end apart: 53 -> 53, of which waited for: 16 -> 16; matrix products, arithmetic and copies ran while one was open for 0% -> 0% of each run, Pallas kernels for 45% -> 46%
where the time goes in v2:
time: 149 us
  Pallas kernels  78.3 us (53%)
  starting transfers between devices  40.3 us (27%)
  waiting for transfers between devices  25.7 us (17%)
  local copies, waits for them, and re-layouts  3.28 us (2%)
    pallas_call x30, Pallas kernels, whole_call(): pl.pallas_call(body, out_shape=kinds, in_specs=[smem_spec] * len(smem) +...  78.3 us
    ppermute x11, starting transfers between devices, dp_swap(): return lax.ppermute(value, 'dp', [(i, i ^ stride) for i in range(dp_size)])  16 us
    ppermute x12, starting transfers between devices, chip_hop(): lax.ppermute(value, 'tensor', [(t, (t // 2 + k) % chips * 2 + t % 2) for...  14.7 us
    ppermute x12, waiting for transfers between devices, chip_hop(): lax.ppermute(value, 'tensor', [(t, (t // 2 + k) % chips * 2 + t % 2) for...  12.3 us
    ppermute x11, waiting for transfers between devices, dp_swap(): return lax.ppermute(value, 'dp', [(i, i ^ stride) for i in range(dp_size)])  12.1 us
    ppermute x24, starting transfers between devices, core_swap(): return lax.ppermute(value, 'tensor', core_perm)  4.51 us
    unnamed x38, local copies, waits for them, and re-layouts  3.06 us
  transfers between devices with their start and end apart: 53, of which 16 were waited for; matrix products, arithmetic and copies ran while one was open for 0% of the time, Pallas kernels for 46%

profile of v2, /device:TPU:0, one launch (start us, length us, event | category | flops | bytes accessed | tf_op | source)
XLA Modules:
  0.0 149.1 jit_solution(9980694368555645076)
XLA Ops:
  1.2 2.6 %collective-permute-start.1 = (bf16[256,1024]{1,0:T(8,128)(2,1)}, bf16[256,1024]{1,0:T(8,128)(2,1)S(1)}, u32[]{:S(2)}, u32[]{:S(2)}) collective-permute-start(bf16[256,1024]{1,0:T(8,128)(2,1)} %tokens.1), channel_id=1, source_target_pairs={{0,2},{1,3},{2,0},{3,1},{4,6},{5,7},{6,4},{7,5},{8,10},{9,11},{10,... | collective-permute-start | bytes 1572872 | tf_op jit(solution)/shard_map/ppermute | solution.py:690
  5.0 3.9 %prep.1 = (bf16[32,1024]{1,0:T(8,128)(2,1)S(1)}, bf16[3,32,256]{2,1,0:T(8,128)(2,1)S(1)}, bf16[272,1024]{1,0:T(8,128)(2,1)S(1)}, bf16[32,1024]{1,0:T(8,128)(2,1)...) custom-call(s32[1]{0:T(128)} %bitcast.me.refs_0_, ...), custom_call_target="tpu_custom_call" | custom-call | tf_op jit(solution)/shard_map/prep/pallas_call | solution.py:46
  9.8 6.2 %qkv_near.1 = (bf16[512,1024]{1,0:T(8,128)(2,1)S(1)}, bf16[512,32]{1,0:T(8,128)(2,1)S(1)}, f32[1024,768]{1,0:T(8,128)S(1)}) custom-call(f32[1024,32]{1,0:T(8,128)S(1)} %get-tuple-element.184.mask, f32[1,1024]{1,0:T(1,128)} %bitcast.28, f32[1,1024]{1,0:T(1,128)} %bitcast.31, bf16[3,1024,256]{2,1,0:T(8,128)(2,1)} %bitcast.12, f32[2,256]{1,0:T(2,128)} %bias.3, ...), custom_call_target="tpu_custom_call" | custom-call | tf_op jit(solution)/shard_map/qkv_near/pallas_call | solution.py:46
  16.5 1.8 %collective-permute-start.4 = (bf16[144,1024]{1,0:T(8,128)(2,1)S(1)}, bf16[144,1024]{1,0:T(8,128)(2,1)S(1)}, u32[]{:S(2)}, u32[]{:S(2)}) collective-permute-start(bf16[144,1024]{1,0:T(8,128)(2,1)S(1)} %get-tuple-element.163), channel_id=1, source_target_pairs={{0,2},{1,3},{2,0},{3,1},{4,6},{5,7},{6,4},{7,5},{8,10},{9,11},{10,... | collective-permute-start | bytes 884744 | tf_op jit(solution)/shard_map/ppermute | solution.py:690
  18.6 4.4 %qkv_far.1 = (bf16[512,1024]{1,0:T(8,128)(2,1)S(1)}, bf16[512,32]{1,0:T(8,128)(2,1)S(1)}, bf16[1024,768]{1,0:T(8,128)(2,1)S(1)}) custom-call(f32[1024,32]{1,0:T(8,128)S(1)} %get-tuple-element.184.mask, f32[1,1024]{1,0:T(1,128)S(1)} %bitcast.29, f32[1,1024]{1,0:T(1,128)S(1)} %bitcast.32, bf16[3,1024,256]{2,1,0:T(8,128)(2,1)S(1)} %bitcast.13, ...), custom_call_target="tpu_custom_call" | custom-call | tf_op jit(solution)/shard_map/qkv_far/pallas_call | solution.py:46
  24.6 4.4 %attend0.1 = (bf16[1024,128]{1,0:T(8,128)(2,1)S(1)}, bf16[2,2,512,512]{3,2,1,0:T(8,128)(2,1)S(1)}) custom-call(s32[1,1024]{1,0:T(1,128)S(1)} %get-tuple-element.164.limit, bf16[1024,768]{1,0:T(8,128)(2,1)S(1)} %get-tuple-element.167.seq.refs_0_.refs_1_, bf16[1024,1024]{1,0:T(8,128)(2,1)S(1)} %get-tuple-element.161.push.refs_4_), custom_call_target="tpu_custom_call" | custom-call | tf_op jit(solution)/shard_map/attend0/pallas_call | solution.py:46
  29.0 4.4 %attend1.1 = (bf16[1024,128]{1,0:T(8,128)(2,1)S(1)}, bf16[2,2,512,512]{3,2,1,0:T(8,128)(2,1)S(1)}) custom-call(s32[1,1024]{1,0:T(1,128)S(1)} %get-tuple-element.164.limit, bf16[1024,768]{1,0:T(8,128)(2,1)S(1)} %get-tuple-element.167.seq.refs_0_.refs_1_, bf16[1024,1024]{1,0:T(8,128)(2,1)S(1)} %get-tuple-element.161.push.refs_4_), custom_call_target="tpu_custom_call" | custom-call | tf_op jit(solution)/shard_map/attend1/pallas_call | solution.py:46
  35.6 6.0 %collective-permute-done.5.refs_3_ = bf16[128,1024]{1,0:T(8,128)(2,1)S(1)} collective-permute-done((bf16[128,1024]{1,0:T(8,128)(2,1)S(1)}, bf16[128,1024]{1,0:T(8,128)(2,1)S(1)}, u32[]{:S(2)}, u32[]{:S(2)}) %collective-permute-start.5) | collective-permute-done | bytes 262176 | tf_op jit(solution)/shard_map/ppermute | solution.py:724
  44.2 5.2 %collective-permute-done.13.refs_7_.refs_9_.refs_5_ = bf16[1024,128]{1,0:T(8,128)(2,1)S(1)} collective-permute-done((bf16[1024,128]{1,0:T(8,128)(2,1)S(1)}, bf16[1024,128]{1,0:T(8,128)(2,1)S(1)}, u32[]{:S(2)}, u32[]{:S(2)}) %collective-permute-start.13) | collective-permute-done | bytes 262176 | tf_op jit(solution)/shard_map/ppermute | solution.py:690
  52.2 5.2 %block_odd.1 = (bf16[256,1024]{1,0:T(8,128)(2,1)S(1)}, bf16[256,1024]{1,0:T(8,128)(2,1)S(1)}, bf16[256,32]{1,0:T(8,128)(2,1)S(1)}, bf16[256,32]{1,0:T(8,128)(2,1...) custom-call(f32[1024,32]{1,0:T(8,128)S(1)} %get-tuple-element.184.ma, ...), custom_call_target="tpu_custom_call" | custom-call | tf_op jit(solution)/shard_map/block_odd/pallas_call | solution.py:46
  58.1 5.1 %block_even.1 = (bf16[256,1024]{1,0:T(8,128)(2,1)S(1)}, bf16[256,1024]{1,0:T(8,128)(2,1)S(1)}, bf16[256,32]{1,0:T(8,128)(2,1)S(1)}, bf16[256,32]{1,0:T(8,128)(2,...) custom-call(f32[1024,32]{1,0:T(8,128)S(1)} %get-tuple-element.184.ma, ...), custom_call_target="tpu_custom_call" | custom-call | tf_op jit(solution)/shard_map/block_even/pallas_call | solution.py:46
  64.3 10.5 %block_near.1 = (bf16[512,1024]{1,0:T(8,128)(2,1)S(1)}, bf16[512,1024]{1,0:T(8,128)(2,1)S(1)}, bf16[512,32]{1,0:T(8,128)(2,1)S(1)}, bf16[512,32]{1,0:T(8,128)(2,...) custom-call(f32[1024,32]{1,0:T(8,128)S(1)} %get-tuple-element.184.ma, ...), custom_call_target="tpu_custom_call" | custom-call | tf_op jit(solution)/shard_map/block_near/pallas_call | solution.py:46
  77.6 2.2 %mid_back.1 = (f32[256,1024]{1,0:T(8,128)S(1)}, bf16[256,1024]{1,0:T(8,128)(2,1)S(1)}, bf16[256,32]{1,0:T(8,128)(2,1)S(1)}, bf16[256,256]{1,0:T(8,128)(2,1)S(1)}...) custom-call(f32[1024,32]{1,0:T(8,128)S(1)} %get-tuple-element.184.mask, ...), custom_call_target="tpu_custom_call" | custom-call | tf_op jit(solution)/shard_map/mid_back/pallas_call | solution.py:46
  82.2 3.1 %down.1 = (bf16[512,1024]{1,0:T(8,128)(2,1)S(1)}, bf16[256,1024]{1,0:T(8,128)(2,1)S(1)}, bf16[256,1024]{1,0:T(8,128)(2,1)S(1)}) custom-call(bf16[1024,1024]{1,0:T(8,128)(2,1)S(1)} %copy-done, bf16[32,1024]{1,0:T(8,128)(2,1)S(1)} %get-tuple-element.176.down_out, bf16[512,1024]{1,0:T(8,128)(2,1)S(1)} %get-tuple-element.196.refs_9_.refs_0_, ...), custom_call_target="tpu_custom_call" | custom-call | tf_op jit(solution)/shard_map/down/pallas_call | solution.py:46
  85.3 2.7 %collective-permute-start.29 = (bf16[32,2176]{1,0:T(8,128)(2,1)S(1)}, bf16[32,2176]{1,0:T(8,128)(2,1)S(1)}, u32[]{:S(2)}, u32[]{:S(2)}) collective-permute-start(bf16[32,2176]{1,0:T(8,128)(2,1)S(1)} %get-tuple-element.244), channel_id=1, source_target_pairs={{0,16},{4,20},{8,24},{12,28},{16,0},{20,4},{24,8},{28,12},{1,17},{... | collective-permute-start | bytes 417800 | tf_op jit(solution)/shard_map/ppermute | solution.py:724
  90.6 4.7 %attend_back0.1 = (bf16[128,1024]{1,0:T(8,128)(2,1)S(1)}, bf16[1024,128]{1,0:T(8,128)(2,1)S(1)}, bf16[1024,128]{1,0:T(8,128)(2,1)S(1)}, bf16[1024,256]{1,0:T(8,128)(2,1)S(1)}) custom-call(bf16[1024,768]{1,0:T(8,128)(2,1)S(1)} %get-tuple-element.167.seq.refs_0_.refs_1_, bf16[2,2,512,512]{3,2,1,0:T(8,128)(2,1)S(1)} %get-tuple-element.227.refs_1_, ...), custom_call_target="tpu_custom_call" | custom-call | tf_op jit(solution)/shard_map/attend_back0/pallas_call | solution.py:46
  99.5 2.7 %collective-permute-start.30 = (bf16[32,1152]{1,0:T(8,128)(2,1)S(1)}, bf16[32,1152]{1,0:T(8,128)(2,1)S(1)}, u32[]{:S(2)}, u32[]{:S(2)}) collective-permute-start(bf16[32,1152]{1,0:T(8,128)(2,1)S(1)} %pack_wide.1), channel_id=1, source_target_pairs={{0,16},{4,20},{8,24},{12,28},{16,0},{20,4},{24,8},{28,12},{1,17},{... | collective-permute-start | bytes 221192 | tf_op jit(solution)/shard_map/ppermute | solution.py:724
  102.2 5.7 %attend_back1.1 = (bf16[256,1024]{1,0:T(8,128)(2,1)S(1)}, bf16[1024,256]{1,0:T(8,128)(2,1)S(1)}, bf16[1024,256]{1,0:T(8,128)(2,1)S(1)}, bf16[32,1024]{1,0:T(8,12...) custom-call(s32[1]{0:T(128)} %bitcast.me.refs_0_, ...), custom_call_target="tpu_custom_call" | custom-call | tf_op jit(solution)/shard_map/attend_back1/pallas_call | solution.py:46
  107.9 1.7 %qkv_back_odd.1 = bf16[256,1024]{1,0:T(8,128)(2,1)S(1)} custom-call(bf16[1024,1024]{1,0:T(8,128)(2,1)S(1)} %get-tuple-element.161.push.refs_4_, bf16[1024,768]{1,0:T(8,128)(2,1)S(1)} %get-tuple-element.254.w_cat, bf16[32,1024]{1,0:T(8,128)(2,1)S(1)} %get-tuple-element.153.low_in, bf16[256,1024]{1,0:T(8,128)(2,1)S(1)} %get-tuple-element.255.grad_q, ...), custom_call_target="tpu_custom_call" | custom-call | tf_op jit(solution)/shard_map/qkv_back_odd/pallas_call | solution.py:46
  119.8 3.5 %qkv_back_near.1.refs_0_ = bf16[512,1024]{1,0:T(8,128)(2,1)S(1)} custom-call(bf16[1024,1024]{1,0:T(8,128)(2,1)S(1)} %get-tuple-element.161.push.refs_4_, bf16[1024,768]{1,0:T(8,128)(2,1)S(1)} %get-tuple-element.254.w_cat, bf16[32,1024]{1,0:T(8,128)(2,1)S(1)} %get-tuple-element.153.low_in, bf16[256,1024]{1,0:T(8,128)(2,1)S(1)} %get-tuple-element.255.grad_q, ...), custom_call_target="tpu_custom_call" | custom-call | tf_op jit(solution)/shard_map/qkv_back_near/pallas_call | solution.py:46
  126.7 3.2 %collective-permute-done.44 = bf16[64,1152]{1,0:T(8,128)(2,1)S(1)} collective-permute-done((bf16[64,1152]{1,0:T(8,128)(2,1)S(1)}, bf16[64,1152]{1,0:T(8,128)(2,1)S(1)}, u32[]{:S(2)}, u32[]{:S(2)}) %collective-permute-start.44) | collective-permute-done | bytes 147488 | tf_op jit(solution)/shard_map/ppermute | solution.py:724
  129.9 2.5 %collective-permute-done.39.refs_3_ = bf16[128,1024]{1,0:T(8,128)(2,1)S(1)} collective-permute-done((bf16[128,1024]{1,0:T(8,128)(2,1)S(1)}, bf16[128,1024]{1,0:T(8,128)(2,1)S(1)}, u32[]{:S(2)}, u32[]{:S(2)}) %collective-permute-start.39) | collective-permute-done | bytes 262176 | tf_op jit(solution)/shard_map/ppermute | solution.py:690
  137.2 1.9 %input_back.1 = f32[256,1024]{1,0:T(8,128)} custom-call(bf16[256,1024]{1,0:T(8,128)(2,1)S(1)} %copy-done.3, f32[256,1024]{1,0:T(8,128)S(1)} %get-tuple-element.280.grad_mid, f32[1,1024]{1,0:T(1,128)S(1)} %bitcast.30, bf16[512,1024]{1,0:T(8,128)(2,1)S(1)} %qkv_back_near.1.refs_0_, bf16[256,1024]{1,0:T(8,128)(2,1)S(1)} %collective-permute-done.46.refs_1_, ...), custom_call_target="tpu_custom_call" | custom-call | tf_op jit(solution)/shard_map/input_back/pallas_call | solution.py:46
  139.4 2.2 %collective-permute-done.45 = bf16[128,1152]{1,0:T(8,128)(2,1)S(1)} collective-permute-done((bf16[128,1152]{1,0:T(8,128)(2,1)S(1)}, bf16[128,1152]{1,0:T(8,128)(2,1)S(1)}, u32[]{:S(2)}, u32[]{:S(2)}) %collective-permute-start.45) | collective-permute-done | bytes 294944 | tf_op jit(solution)/shard_map/ppermute | solution.py:724
  (166 shorter events, 52.1 us)
Async XLA Ops:
  0.6 8.3 %collective-permute-start = (bf16[256,1024]{1,0:T(8,128)(2,1)}, bf16[256,1024]{1,0:T(8,128)(2,1)S(1)}, u32[]{:S(2)}, u32[]{:S(2)}) collective-permute-start(bf16[256,1024]{1,0:T(8,128)(2,1)} %tokens.1), channel_id=1, source_target_pairs={{0,1},{1,0},{2,3},{3,2},{4,5},{5,4},{6,7},{7,6},{8,9},{9,8},{10,11... | collective-permute-start | bytes 1572872 | tf_op jit(solution)/shard_map/ppermute | solution.py:687
  1.2 15.3 %collective-permute-start.1 = (bf16[256,1024]{1,0:T(8,128)(2,1)}, bf16[256,1024]{1,0:T(8,128)(2,1)S(1)}, u32[]{:S(2)}, u32[]{:S(2)}) collective-permute-start(bf16[256,1024]{1,0:T(8,128)(2,1)} %tokens.1), channel_id=1, source_target_pairs={{0,2},{1,3},{2,0},{3,1},{4,6},{5,7},{6,4},{7,5},{8,10},{9,11},{10,... | collective-permute-start | bytes 1572872 | tf_op jit(solution)/shard_map/ppermute | solution.py:690
  16.5 17.0 %collective-permute-start.4 = (bf16[144,1024]{1,0:T(8,128)(2,1)S(1)}, bf16[144,1024]{1,0:T(8,128)(2,1)S(1)}, u32[]{:S(2)}, u32[]{:S(2)}) collective-permute-start(bf16[144,1024]{1,0:T(8,128)(2,1)S(1)} %get-tuple-element.163), channel_id=1, source_target_pairs={{0,2},{1,3},{2,0},{3,1},{4,6},{5,7},{6,4},{7,5},{8,10},{9,11},{10,... | collective-permute-start | bytes 884744 | tf_op jit(solution)/shard_map/ppermute | solution.py:690
  18.2 24.0 %collective-permute-start.3 = (bf16[272,1024]{1,0:T(8,128)(2,1)S(1)}, bf16[272,1024]{1,0:T(8,128)(2,1)S(1)}, u32[]{:S(2)}, u32[]{:S(2)}) collective-permute-start(bf16[272,1024]{1,0:T(8,128)(2,1)S(1)} %get-tuple-element.162.refs_0_), channel_id=1, source_target_pairs={{0,1},{1,0},{2,3},{3,2},{4,5},{5,4},{6,7},{7,6},{8,9},{9,8},{10,11... | collective-permute-start | bytes 1671176 | tf_op jit(solution)/shard_map/ppermute | solution.py:687
  23.0 19.3 %collective-permute-start.8 = (bf16[256,1024]{1,0:T(8,128)(2,1)S(1)}, bf16[256,1024]{1,0:T(8,128)(2,1)S(1)}, u32[]{:S(2)}, u32[]{:S(2)}) collective-permute-start(bf16[256,1024]{1,0:T(8,128)(2,1)S(1)} %convert_element_type.3.refs_2_.refs_21_), channel_id=1, source_target_pairs={{0,2},{1,3},{2,0},{3,1},{4,6},{5,7},{6,4},{7,5},{8,10},{9,11},{10,... | collective-permute-start | bytes 1572872 | tf_op jit(solution)/shard_map/ppermute | solution.py:690
  33.5 8.1 %collective-permute-start.5 = (bf16[128,1024]{1,0:T(8,128)(2,1)S(1)}, bf16[128,1024]{1,0:T(8,128)(2,1)S(1)}, u32[]{:S(2)}, u32[]{:S(2)}) collective-permute-start(bf16[128,1024]{1,0:T(8,128)(2,1)S(1)} %slice.24), channel_id=1, source_target_pairs={{0,4},{4,0},{8,12},{12,8},{16,20},{20,16},{24,28},{28,24},{1,5},{5... | collective-permute-start | bytes 786440 | tf_op jit(solution)/shard_map/ppermute | solution.py:724
  35.1 14.3 %collective-permute-start.6 = (bf16[144,1024]{1,0:T(8,128)(2,1)S(1)}, bf16[144,1024]{1,0:T(8,128)(2,1)S(1)}, u32[]{:S(2)}, u32[]{:S(2)}) collective-permute-start(bf16[144,1024]{1,0:T(8,128)(2,1)S(1)} %collective-permute-done.4.refs_2_), channel_id=1, source_target_pairs={{0,1},{1,0},{2,3},{3,2},{4,5},{5,4},{6,7},{7,6},{8,9},{9,8},{10,11... | collective-permute-start | bytes 884744 | tf_op jit(solution)/shard_map/ppermute | solution.py:687
  35.1 9.1 %collective-permute-start.12 = (bf16[1024,128]{1,0:T(8,128)(2,1)S(1)}, bf16[1024,128]{1,0:T(8,128)(2,1)S(1)}, u32[]{:S(2)}, u32[]{:S(2)}) collective-permute-start(bf16[1024,128]{1,0:T(8,128)(2,1)S(1)} %get-tuple-element.166.refs_2_.refs_4_.refs_0_), channel_id=1, source_target_pairs={{0,2},{1,3},{2,0},{3,1},{4,6},{5,7},{6,4},{7,5},{8,10},{9,11},{10,... | collective-permute-start | bytes 786440 | tf_op jit(solution)/shard_map/ppermute | solution.py:690
  42.3 9.5 %collective-permute-start.9 = (bf16[256,1024]{1,0:T(8,128)(2,1)S(1)}, bf16[256,1024]{1,0:T(8,128)(2,1)S(1)}, u32[]{:S(2)}, u32[]{:S(2)}) collective-permute-start(bf16[256,1024]{1,0:T(8,128)(2,1)S(1)} %collective-permute-done.8.refs_1_.refs_23_), channel_id=1, source_target_pairs={{0,1},{1,0},{2,3},{3,2},{4,5},{5,4},{6,7},{7,6},{8,9},{9,8},{10,11... | collective-permute-start | bytes 1572872 | tf_op jit(solution)/shard_map/ppermute | solution.py:687
  63.3 14.3 %collective-permute-start.19 = (bf16[256,1024]{1,0:T(8,128)(2,1)S(1)}, bf16[256,1024]{1,0:T(8,128)(2,1)S(1)}, u32[]{:S(2)}, u32[]{:S(2)}) collective-permute-start(bf16[256,1024]{1,0:T(8,128)(2,1)S(1)} %up_join.1), channel_id=1, source_target_pairs={{0,2},{1,3},{2,0},{3,1},{4,6},{5,7},{6,4},{7,5},{8,10},{9,11},{10,... | collective-permute-start | bytes 1572872 | tf_op jit(solution)/shard_map/ppermute | solution.py:690
  79.9 8.1 %collective-permute-start.20 = (bf16[256,256]{1,0:T(8,128)(2,1)S(1)}, bf16[256,256]{1,0:T(8,128)(2,1)S(1)}, u32[]{:S(2)}, u32[]{:S(2)}) collective-permute-start(bf16[256,256]{1,0:T(8,128)(2,1)S(1)} %get-tuple-element.217), channel_id=1, source_target_pairs={{0,1},{1,0},{2,3},{3,2},{4,5},{5,4},{6,7},{7,6},{8,9},{9,8},{10,11... | collective-permute-start | bytes 393224 | tf_op jit(solution)/shard_map/ppermute | solution.py:687
  79.9 8.0 %collective-permute-start.21 = (bf16[256,256]{1,0:T(8,128)(2,1)S(1)}, bf16[256,256]{1,0:T(8,128)(2,1)S(1)}, u32[]{:S(2)}, u32[]{:S(2)}) collective-permute-start(bf16[256,256]{1,0:T(8,128)(2,1)S(1)} %get-tuple-element.219), channel_id=1, source_target_pairs={{0,2},{1,3},{2,0},{3,1},{4,6},{5,7},{6,4},{7,5},{8,10},{9,11},{10,... | collective-permute-start | bytes 393224 | tf_op jit(solution)/shard_map/ppermute | solution.py:706
  85.3 10.1 %collective-permute-start.29 = (bf16[32,2176]{1,0:T(8,128)(2,1)S(1)}, bf16[32,2176]{1,0:T(8,128)(2,1)S(1)}, u32[]{:S(2)}, u32[]{:S(2)}) collective-permute-start(bf16[32,2176]{1,0:T(8,128)(2,1)S(1)} %get-tuple-element.244), channel_id=1, source_target_pairs={{0,16},{4,20},{8,24},{12,28},{16,0},{20,4},{24,8},{28,12},{1,17},{... | collective-permute-start | bytes 417800 | tf_op jit(solution)/shard_map/ppermute | solution.py:724
  95.4 12.5 %collective-permute-start.32 = (bf16[64,2176]{1,0:T(8,128)(2,1)S(1)}, bf16[64,2176]{1,0:T(8,128)(2,1)S(1)}, u32[]{:S(2)}, u32[]{:S(2)}) collective-permute-start(bf16[64,2176]{1,0:T(8,128)(2,1)S(1)} %get-tuple-element.295), channel_id=1, source_target_pairs={{0,4},{4,0},{8,12},{12,8},{16,20},{20,16},{24,28},{28,24},{1,5},{5... | collective-permute-start | bytes 835592 | tf_op jit(solution)/shard_map/ppermute | solution.py:724
  96.4 11.5 %collective-permute-start.31 = (bf16[64,2176]{1,0:T(8,128)(2,1)S(1)}, bf16[64,2176]{1,0:T(8,128)(2,1)S(1)}, u32[]{:S(2)}, u32[]{:S(2)}) collective-permute-start(bf16[64,2176]{1,0:T(8,128)(2,1)S(1)} %get-tuple-element.295), channel_id=1, source_target_pairs={{0,8},{4,12},{8,0},{12,4},{16,24},{20,28},{24,16},{28,20},{1,9},{5... | collective-permute-start | bytes 835592 | tf_op jit(solution)/shard_map/ppermute | solution.py:724
  98.1 9.8 %collective-permute-start.28 = (bf16[128,1024]{1,0:T(8,128)(2,1)S(1)}, bf16[128,1024]{1,0:T(8,128)(2,1)S(1)}, u32[]{:S(2)}, u32[]{:S(2)}) collective-permute-start(bf16[128,1024]{1,0:T(8,128)(2,1)S(1)} %slice.32), channel_id=1, source_target_pairs={{0,2},{1,3},{2,0},{3,1},{4,6},{5,7},{6,4},{7,5},{8,10},{9,11},{10,... | collective-permute-start | bytes 786440 | tf_op jit(solution)/shard_map/ppermute | solution.py:690
  99.5 8.4 %collective-permute-start.30 = (bf16[32,1152]{1,0:T(8,128)(2,1)S(1)}, bf16[32,1152]{1,0:T(8,128)(2,1)S(1)}, u32[]{:S(2)}, u32[]{:S(2)}) collective-permute-start(bf16[32,1152]{1,0:T(8,128)(2,1)S(1)} %pack_wide.1), channel_id=1, source_target_pairs={{0,16},{4,20},{8,24},{12,28},{16,0},{20,4},{24,8},{28,12},{1,17},{... | collective-permute-start | bytes 221192 | tf_op jit(solution)/shard_map/ppermute | solution.py:724
  112.6 11.6 %collective-permute-start.43 = (bf16[64,2176]{1,0:T(8,128)(2,1)S(1)}, bf16[64,2176]{1,0:T(8,128)(2,1)S(1)}, u32[]{:S(2)}, u32[]{:S(2)}) collective-permute-start(bf16[64,2176]{1,0:T(8,128)(2,1)S(1)} %collective-permute-done.31), channel_id=1, source_target_pairs={{0,4},{4,0},{8,12},{12,8},{16,20},{20,16},{24,28},{28,24},{1,5},{5... | collective-permute-start | bytes 835592 | tf_op jit(solution)/shard_map/ppermute | solution.py:724
  116.2 8.0 %collective-permute-start.38 = (bf16[128,1024]{1,0:T(8,128)(2,1)S(1)}, bf16[128,1024]{1,0:T(8,128)(2,1)S(1)}, u32[]{:S(2)}, u32[]{:S(2)}) collective-permute-start(bf16[128,1024]{1,0:T(8,128)(2,1)S(1)} %slice.33), channel_id=1, source_target_pairs={{0,2},{1,3},{2,0},{3,1},{4,6},{5,7},{6,4},{7,5},{8,10},{9,11},{10,... | collective-permute-start | bytes 786440 | tf_op jit(solution)/shard_map/ppermute | solution.py:690
  117.0 29.9 %collective-permute-start.23 = (bf16[256,1024]{1,0:T(8,128)(2,1)S(1)}, bf16[256,1024]{1,0:T(8,128)(2,1)S(1)}, u32[]{:S(2)}, u32[]{:S(2)}) collective-permute-start(bf16[256,1024]{1,0:T(8,128)(2,1)S(1)} %slice.26), channel_id=1, source_target_pairs={{0,1},{1,0},{2,3},{3,2},{4,5},{5,4},{6,7},{7,6},{8,9},{9,8},{10,11... | collective-permute-start | bytes 1572872 | tf_op jit(solution)/shard_map/ppermute | solution.py:687
  118.6 13.8 %collective-permute-start.41 = (bf16[128,1152]{1,0:T(8,128)(2,1)S(1)}, bf16[128,1152]{1,0:T(8,128)(2,1)S(1)}, u32[]{:S(2)}, u32[]{:S(2)}) collective-permute-start(bf16[128,1152]{1,0:T(8,128)(2,1)S(1)} %pad_maximum_fusion.2), channel_id=1, source_target_pairs={{0,4},{4,0},{8,12},{12,8},{16,20},{20,16},{24,28},{28,24},{1,5},{5... | collective-permute-start | bytes 884744 | tf_op jit(solution)/shard_map/ppermute | solution.py:724
  126.6 9.2 %collective-permute-start.46 = (bf16[256,1024]{1,0:T(8,128)(2,1)S(1)}, bf16[256,1024]{1,0:T(8,128)(2,1)S(1)}, u32[]{:S(2)}, u32[]{:S(2)}) collective-permute-start(bf16[256,1024]{1,0:T(8,128)(2,1)S(1)} %slice.34), channel_id=1, source_target_pairs={{0,1},{1,0},{2,3},{3,2},{4,5},{5,4},{6,7},{7,6},{8,9},{9,8},{10,11... | collective-permute-start | bytes 1572872 | tf_op jit(solution)/shard_map/ppermute | solution.py:687
  135.7 8.9 %collective-permute-start.47 = (bf16[384,256]{1,0:T(8,128)(2,1)S(1)}, bf16[384,256]{1,0:T(8,128)(2,1)S(1)}, u32[]{:S(2)}, u32[]{:S(2)}) collective-permute-start(bf16[384,256]{1,0:T(8,128)(2,1)S(1)} %get-tuple-element.285.refs_0_), channel_id=1, source_target_pairs={{0,1},{1,0},{2,3},{3,2},{4,5},{5,4},{6,7},{7,6},{8,9},{9,8},{10,11... | collective-permute-start | bytes 589832 | tf_op jit(solution)/shard_map/ppermute | solution.py:687
  135.8 11.1 %collective-permute-start.40 = (bf16[128,1024]{1,0:T(8,128)(2,1)S(1)}, bf16[128,1024]{1,0:T(8,128)(2,1)S(1)}, u32[]{:S(2)}, u32[]{:S(2)}) collective-permute-start(bf16[128,1024]{1,0:T(8,128)(2,1)S(1)} %slice.30), channel_id=1, source_target_pairs={{0,2},{1,3},{2,0},{3,1},{4,6},{5,7},{6,4},{7,5},{8,10},{9,11},{10,... | collective-permute-start | bytes 786440 | tf_op jit(solution)/shard_map/ppermute | solution.py:690
  (46 other events, 259.7 us)
